TPU v7x, 32 devices: a whole 2x2x4 slice. The times are simulated.
32 devices in a mesh: tx: 4 (over z), ty: 8 (over y, x, core).
Axes of the slice: x: 2, y: 2, z: 4, core: 2. Of those that a mesh axis runs over, the one named last changes fastest.
Arguments:
- frames: bfloat16 [4, 24, 1, 5, 384, 384], P('tx', 'ty'), may hold values from -6 to 6
- masks: int32 [4, 24, 12, 12], P('tx', 'ty'), may hold values 0 or 1
- phases: float32 [4, 24, 1], P('tx', 'ty'), may hold values from -3.140625 to 3.140625
- slot_tile: int32 [4, 24], P('tx', 'ty'), may hold values from -1 to 15, as said below
- otf: float32 [384, 384], replicated, may hold values from 0.05 to 1
- apod: float32 [384, 384], replicated, may hold values from 0.2 to 1
Outputs:
- stitched: float32 [2560, 2560], P('ty', 'tx')
Inputs may be any that keep to these rules, and one draw needn't show every extreme that they name: `slot_tile`: in each column of devices, every tile is held in exactly one slot and is named 2 h + c for its tile row h and its tile column c within that column of devices; -1 marks an empty slot. The slots of one device never hold two tiles of the same tile row. In every draw some devices of every column hold 3 tiles.
All inputs are finite; a program needn't handle non-finite values. No bound on the sum of `masks` on one device may be relied on, other than what follows from the above.
Results may differ from a plain program's by a relative error of at most 0.0068.
Values may be sent and summed in bfloat16 or wider, within the bound.
A program may use at most 128 MiB of HBM per device.

v0:
```python
import math

import jax
import jax.numpy as jnp
from jax import lax
from jax.sharding import PartitionSpec as P

STRIDE = 320
GROUP_COLS = 2


wiener = 0.1
pattern_base = (37, 101)
pattern_step = (29, -53)


def passed_along(value, axis, steps):
    count = lax.axis_size(axis)
    leading, last = (max(0, -steps), min(count, count - steps))
    return lax.ppermute(value, axis, [(source, source + steps) for source in range(leading, last)])


def batched(pattern, operand_a, operand_b):
    return jnp.einsum(pattern, operand_a, operand_b, preferred_element_type=jnp.float32)


def plain_dot(operand_a, operand_b):
    return jnp.dot(operand_a, operand_b, preferred_element_type=jnp.float32)


def mix_bands(pattern, operand_a, operand_b):
    return jnp.einsum(pattern, operand_a, operand_b, precision=lax.Precision.HIGHEST)


def dft_tables(length):
    places = jnp.arange(length, dtype=jnp.int32)
    product = places[:, None] * places[None, :] % length
    angles = product.astype(jnp.float32) * (2.0 * math.pi / length)
    return (jnp.cos(angles).astype(jnp.bfloat16), jnp.sin(angles).astype(jnp.bfloat16))


def pattern_shift(orient):
    return (pattern_base[0] + orient * pattern_step[0], pattern_base[1] + orient * pattern_step[1])


def filter_weights(otf, apod, phase_count):
    halfway = phase_count // 2
    rolled = []
    shift_rows, shift_cols = pattern_shift(0)
    for band_place in range(phase_count):
        band_order = band_place - halfway
        rolled.append(jnp.roll(otf, (-band_order * shift_rows, -band_order * shift_cols), (0, 1)))
    rolled_stack = jnp.stack(rolled)
    denominator = wiener + jnp.sum(rolled_stack * rolled_stack, axis=0)
    return rolled_stack * (apod / denominator)[None]


def tile_image(planes, cell_mask, offsets, gain_maps, cosine, sine_table):
    orient_count, phase_count, length = (planes.shape[0], planes.shape[1], planes.shape[2])
    cell_count = cell_mask.shape[0]
    cell_width = length // cell_count
    shaped = planes.reshape(
        orient_count * phase_count, cell_count, cell_width, cell_count, cell_width
    )
    masked = (shaped * cell_mask.astype(jnp.bfloat16)[None, :, None, :, None]).reshape(
        orient_count * phase_count, length, length
    )
    first_real = batched("pjk,kl->pjl", masked, cosine).astype(jnp.bfloat16)
    first_imag = (-batched("pjk,kl->pjl", masked, sine_table)).astype(jnp.bfloat16)
    four_real = batched("jk,pkl->pjl", cosine, first_real) + batched(
        "jk,pkl->pjl", sine_table, first_imag
    )
    four_imag = batched("jk,pkl->pjl", cosine, first_imag) - batched(
        "jk,pkl->pjl", sine_table, first_real
    )
    halfway = phase_count // 2
    orders = jnp.arange(-halfway, halfway + 1).astype(jnp.float32)
    phase_steps = jnp.arange(phase_count).astype(jnp.float32) * (2.0 * math.pi / phase_count)
    spec_real = jnp.zeros((length, length), jnp.float32)
    spec_imag = jnp.zeros((length, length), jnp.float32)
    shift_rows, shift_cols = pattern_shift(0)
    angles = orders[:, None] * (offsets[0] + phase_steps)[None, :]
    coef_real = jnp.cos(angles) / phase_count
    coef_imag = jnp.sin(angles) / phase_count
    band_real = mix_bands("mp,pxy->mxy", coef_real, four_real) + mix_bands(
        "mp,pxy->mxy", coef_imag, four_imag
    )
    band_imag = mix_bands("mp,pxy->mxy", coef_real, four_imag) - mix_bands(
        "mp,pxy->mxy", coef_imag, four_real
    )
    for band_place in range(phase_count):
        band_order = band_place - halfway
        offset_pair = (-band_order * shift_rows, -band_order * shift_cols)
        gain_map = gain_maps[band_place]
        spec_real = spec_real + gain_map * jnp.roll(band_real[band_place], offset_pair, (0, 1))
        spec_imag = spec_imag + gain_map * jnp.roll(band_imag[band_place], offset_pair, (0, 1))
    wave_real = spec_real.astype(jnp.bfloat16)
    wave_imag = spec_imag.astype(jnp.bfloat16)
    mid_real = (plain_dot(wave_real, cosine) - plain_dot(wave_imag, sine_table)).astype(
        jnp.bfloat16
    )
    mid_imag = (plain_dot(wave_real, sine_table) + plain_dot(wave_imag, cosine)).astype(
        jnp.bfloat16
    )
    return (plain_dot(cosine, mid_real) - plain_dot(sine_table, mid_imag)) * (
        1.0 / (length * length)
    )


def ramp_weights(length, intersection, is_last):
    places = jnp.arange(length).astype(jnp.float32) + 0.5
    rising = jnp.minimum(places / intersection, 1.0)
    falling = jnp.minimum((length - places) / intersection, 1.0)
    return rising * jnp.where(is_last, jnp.ones_like(falling), falling)


def blended(picture, row_last, column_last, intersection):
    length = picture.shape[0]
    weighted = (
        picture
        * ramp_weights(length, intersection, row_last)[:, None]
        * ramp_weights(length, intersection, column_last)[None, :]
    )
    return weighted.astype(jnp.bfloat16)


def fold_rows(padded_block, intersection):
    arrived = passed_along(padded_block[:intersection].astype(jnp.bfloat16), "ty", -1).astype(
        jnp.float32
    )
    interior = padded_block[intersection:]
    keep_rows = interior.shape[0] - intersection
    return jnp.concatenate([interior[:keep_rows], interior[keep_rows:] + arrived], axis=0)


def fold_columns(padded_block, intersection):
    arrived = passed_along(padded_block[:, :intersection].astype(jnp.bfloat16), "tx", -1).astype(
        jnp.float32
    )
    interior = padded_block[:, intersection:]
    keep_cols = interior.shape[1] - intersection
    return jnp.concatenate([interior[:, :keep_cols], interior[:, keep_cols:] + arrived], axis=1)


def shards(frames, masks, phases, slot_tile, otf, apod):
    row_count = lax.axis_size("ty")
    group_count = lax.axis_size("tx")
    my_group = lax.axis_index("tx")
    length = otf.shape[0]
    intersection = length - STRIDE
    cosine, sine_table = dft_tables(length)
    gain_maps = filter_weights(otf, apod, frames.shape[3])
    own_tiles = slot_tile[0]

    def one_slot(slot_items):
        planes, cell_mask, offsets, tile_id = slot_items
        picture = tile_image(planes, cell_mask, offsets, gain_maps, cosine, sine_table)
        tile_row = tile_id // GROUP_COLS
        column = GROUP_COLS * my_group + tile_id % GROUP_COLS
        result = blended(
            picture, tile_row == row_count - 1, column == GROUP_COLS * group_count - 1, intersection
        )
        return jnp.where(tile_id >= 0, result, jnp.zeros_like(result))

    results = lax.map(one_slot, (frames[0], masks[0], phases[0], own_tiles))
    column_places = jnp.arange(GROUP_COLS, dtype=jnp.int32)
    owner_rows = jnp.arange(row_count, dtype=jnp.int32)
    matches = ((own_tiles // GROUP_COLS)[:, None] == owner_rows[None, :]) & (own_tiles >= 0)[
        :, None
    ]
    choose = matches.astype(jnp.bfloat16)
    outgoing = batched("sh,sxy->hxy", choose, results).astype(jnp.bfloat16)
    labels = jnp.sum(matches.astype(jnp.int32) * (own_tiles % GROUP_COLS + 1)[:, None], axis=0) - 1
    incoming, column_tags = (
        lax.all_to_all(outgoing, "ty", split_axis=0, concat_axis=0, tiled=True),
        lax.all_to_all(labels[:, None], "ty", split_axis=0, concat_axis=0, tiled=True),
    )
    selector = (column_tags == column_places[None, :]).astype(jnp.bfloat16)
    tiles_here = batched("sc,sxy->cxy", selector, incoming)
    padded = jnp.zeros((length, STRIDE * GROUP_COLS + intersection), jnp.float32)
    for column_place in range(GROUP_COLS):
        padded = padded + jnp.pad(
            tiles_here[column_place],
            ((0, 0), (STRIDE * column_place, STRIDE * (GROUP_COLS - 1 - column_place))),
        )
    stitched = fold_columns(fold_rows(padded, intersection), intersection)
    return stitched


def solution(mesh):
    in_specs = (
        P("tx", "ty", None, None, None, None),
        P("tx", "ty", None, None),
        P("tx", "ty", None),
        P("tx", "ty"),
        P(),
        P(),
    )
    out_specs = P("ty", "tx")
    return jax.shard_map(shards, mesh=mesh, in_specs=in_specs, out_specs=out_specs, check_vma=False)
```

profile of v0, /device:TPU:0, one launch (start us, length us, event | category | flops | bytes accessed | tf_op | source)
XLA Modules:
  0.0 356.2 jit_solution(4060269184288474588)
XLA Ops:
  2.6 5.2 %all-to-all-start = ((s32[8,1,1]{2,1,0:T(1,128)}), s32[8,1,1]{2,1,0:T(1,128)}, u32[]{:S(2)}, u32[]{:S(2)}) async-start(s32[8,1,1]{2,1,0:T(1,128)} %copy.99), calls=%async_computation | async-start | bytes 8192 | tf_op jit(solution)/shard_map/all_to_all | solution.py:176
  13.2 290.1 %while.14 = (s32[]{:T(128)}, bf16[3,384,384]{1,2,0:T(8,128)(2,1)}, s32[3]{0:T(128)S(1)}, f32[5,384,384]{2,1,0:T(8,128)S(1)}, f32[3,1]{0,1:T(1,128)S(1)}, /*index...) while((s32[]{:T(128)}, bf16[3,384,384]{1,2,0:T(8,128)(2,1)}, ...), condition=%wide.region_3.4_spmd.clone.clone, body=%wide.region_2.3_spmd.clone.clone.sunk | while | flops 4285588224 | bytes 185773616 | solution.py:165
  30.0 4.6 %add_bitcast_fusion.3 = f32[5,384,384]{1,2,0:T(8,128)} fusion(f32[5,384,384]{2,1,0:T(8,128)S(1)} %fusion.243, bf16[5,384,384]{2,1,0:T(8,128)(2,1)S(1)} %negate_convert_fusion.2), kind=kOutput, calls=%fused_computation.5.clone.1 | convolution fusion | flops 568442880 | bytes 7372800 | tf_op jit(solution)/shard_map/while/body/eval_jaxpr/jk,pkl->pjl/dot_general | solution.py:24
  34.7 5.8 %copy.132 = f32[5,384,384]{2,0,1:T(8,128)} copy(f32[5,384,384]{1,2,0:T(8,128)} %add_bitcast_fusion.3) | data formatting | bytes 5898240 | tf_op jit(solution)/shard_map/while/body/eval_jaxpr/add | solution.py:70
  41.7 8.8 %fusion.249 = f32[5,384,384]{2,0,1:T(8,128)} fusion(f32[5,384,384]{2,0,1:T(8,128)} %copy.132, f32[5]{0:T(128)S(1)} %multiply_add_fusion.2, f32[5]{0:T(128)S(1)} %add_convert_fusion.2), kind=kOutput, calls=%fused_computation.121.clone.1 | convolution fusion | flops 44236848 | bytes 5898280 | tf_op jit(solution)/shard_map/while/body/eval_jaxpr/mp,pxy->mxy/dot_general | solution.py:32
  53.5 4.6 %subtract_bitcast_fusion.2 = f32[5,384,384]{1,2,0:T(8,128)} fusion(f32[5,384,384]{2,1,0:T(8,128)S(1)} %fusion.241, bf16[5,384,384]{2,1,0:T(8,128)(2,1)S(1)} %copy-done.1), kind=kOutput, calls=%fused_computation.4.clone.1 | convolution fusion | flops 568442880 | bytes 7372800 | tf_op jit(solution)/shard_map/while/body/eval_jaxpr/jk,pkl->pjl/dot_general | solution.py:24
  58.1 5.4 %copy.131 = f32[5,384,384]{2,0,1:T(8,128)} copy(f32[5,384,384]{1,2,0:T(8,128)} %subtract_bitcast_fusion.2) | data formatting | bytes 5898240 | tf_op jit(solution)/shard_map/while/body/eval_jaxpr/sub | solution.py:73
  63.5 6.3 %fusion.250 = f32[5,384,384]{2,0,1:T(8,128)S(1)} fusion(f32[5,384,384]{2,0,1:T(8,128)} %copy.131, f32[5]{0:T(128)S(1)} %multiply_add_fusion.2, f32[5]{0:T(128)S(1)} %add_convert_fusion.2), kind=kOutput, calls=%fused_computation.117.clone.1 | convolution fusion | flops 44236848 | bytes 5898280 | tf_op jit(solution)/shard_map/while/body/eval_jaxpr/mp,pxy->mxy/dot_general | solution.py:32
  73.8 5.0 %fusion.244 = f32[5,384,384]{2,0,1:T(8,128)S(1)} fusion(f32[5,384,384]{2,0,1:T(8,128)S(1)} %bitcast.249, f32[5]{0:T(128)S(1)} %multiply_add_fusion.2, f32[5]{0:T(128)S(1)} %add_convert_fusion.2), kind=kOutput, calls=%fused_computation.118.clone.1 | convolution fusion | flops 44236848 | bytes 5898280 | tf_op jit(solution)/shard_map/while/body/eval_jaxpr/mp,pxy->mxy/dot_general | solution.py:32
  78.8 5.0 %fusion.242 = f32[5,384,384]{2,0,1:T(8,128)S(1)} fusion(f32[5,384,384]{2,0,1:T(8,128)S(1)} %bitcast.251, f32[5]{0:T(128)S(1)} %multiply_add_fusion.2, f32[5]{0:T(128)S(1)} %add_convert_fusion.2), kind=kOutput, calls=%fused_computation.122.clone.1 | convolution fusion | flops 44236848 | bytes 5898280 | tf_op jit(solution)/shard_map/while/body/eval_jaxpr/mp,pxy->mxy/dot_general | solution.py:32
  90.6 4.8 %fusion.254 = f32[384,384]{1,0:T(8,128)} fusion(f32[384,384]{1,0:T(8,128)} %fusion.248, bf16[384,384]{1,0:T(8,128)(2,1)S(1)} %fusion.253), kind=kOutput, calls=%fused_computation.20.clone.1 | convolution fusion | flops 229736448 | bytes 1474560 | tf_op jit(solution)/shard_map/while/body/eval_jaxpr/dot_general | solution.py:28
  103.8 4.9 %fusion.256 = bf16[3,384,384]{1,2,0:T(8,128)(2,1)} fusion(bf16[3,384,384]{1,2,0:T(8,128)(2,1)} %get-tuple-element.367, s32[]{:T(128)} %get-tuple-element.366, f32[384,384]{1,0:T(8,128)} %fusion.254, f32[384,384]{1,0:T(8,128)} %fusion.255, bf16[384,384]{1,0:T(8,128)(2,1)S(1)} %fusion.253, f32[384]{0:T(512)S(1)} %get-tuple-element.351, ...), kind=kOutput, calls=%fused_computation.19.clone.1 | convolution fusion | flops 230473728 | bytes 1773057 | tf_op jit(solution)/shard_map/while/body/eval_jaxpr/dot_general | solution.py:28
  125.5 4.6 %add_bitcast_fusion.3 = f32[5,384,384]{1,2,0:T(8,128)} fusion(f32[5,384,384]{2,1,0:T(8,128)S(1)} %fusion.243, bf16[5,384,384]{2,1,0:T(8,128)(2,1)S(1)} %negate_convert_fusion.2), kind=kOutput, calls=%fused_computation.5.clone.1 | convolution fusion | flops 568442880 | bytes 7372800 | tf_op jit(solution)/shard_map/while/body/eval_jaxpr/jk,pkl->pjl/dot_general | solution.py:24
  130.1 5.5 %copy.132 = f32[5,384,384]{2,0,1:T(8,128)} copy(f32[5,384,384]{1,2,0:T(8,128)} %add_bitcast_fusion.3) | data formatting | bytes 5898240 | tf_op jit(solution)/shard_map/while/body/eval_jaxpr/add | solution.py:70
  136.9 8.8 %fusion.249 = f32[5,384,384]{2,0,1:T(8,128)} fusion(f32[5,384,384]{2,0,1:T(8,128)} %copy.132, f32[5]{0:T(128)S(1)} %multiply_add_fusion.2, f32[5]{0:T(128)S(1)} %add_convert_fusion.2), kind=kOutput, calls=%fused_computation.121.clone.1 | convolution fusion | flops 44236848 | bytes 5898280 | tf_op jit(solution)/shard_map/while/body/eval_jaxpr/mp,pxy->mxy/dot_general | solution.py:32
  153.3 5.4 %copy.131 = f32[5,384,384]{2,0,1:T(8,128)} copy(f32[5,384,384]{1,2,0:T(8,128)} %subtract_bitcast_fusion.2) | data formatting | bytes 5898240 | tf_op jit(solution)/shard_map/while/body/eval_jaxpr/sub | solution.py:73
  158.6 6.6 %fusion.250 = f32[5,384,384]{2,0,1:T(8,128)S(1)} fusion(f32[5,384,384]{2,0,1:T(8,128)} %copy.131, f32[5]{0:T(128)S(1)} %multiply_add_fusion.2, f32[5]{0:T(128)S(1)} %add_convert_fusion.2), kind=kOutput, calls=%fused_computation.117.clone.1 | convolution fusion | flops 44236848 | bytes 5898280 | tf_op jit(solution)/shard_map/while/body/eval_jaxpr/mp,pxy->mxy/dot_general | solution.py:32
  169.1 5.0 %fusion.244 = f32[5,384,384]{2,0,1:T(8,128)S(1)} fusion(f32[5,384,384]{2,0,1:T(8,128)S(1)} %bitcast.249, f32[5]{0:T(128)S(1)} %multiply_add_fusion.2, f32[5]{0:T(128)S(1)} %add_convert_fusion.2), kind=kOutput, calls=%fused_computation.118.clone.1 | convolution fusion | flops 44236848 | bytes 5898280 | tf_op jit(solution)/shard_map/while/body/eval_jaxpr/mp,pxy->mxy/dot_general | solution.py:32
  174.2 5.0 %fusion.242 = f32[5,384,384]{2,0,1:T(8,128)S(1)} fusion(f32[5,384,384]{2,0,1:T(8,128)S(1)} %bitcast.251, f32[5]{0:T(128)S(1)} %multiply_add_fusion.2, f32[5]{0:T(128)S(1)} %add_convert_fusion.2), kind=kOutput, calls=%fused_computation.122.clone.1 | convolution fusion | flops 44236848 | bytes 5898280 | tf_op jit(solution)/shard_map/while/body/eval_jaxpr/mp,pxy->mxy/dot_general | solution.py:32
  185.7 4.8 %fusion.254 = f32[384,384]{1,0:T(8,128)} fusion(f32[384,384]{1,0:T(8,128)} %fusion.248, bf16[384,384]{1,0:T(8,128)(2,1)S(1)} %fusion.253), kind=kOutput, calls=%fused_computation.20.clone.1 | convolution fusion | flops 229736448 | bytes 1474560 | tf_op jit(solution)/shard_map/while/body/eval_jaxpr/dot_general | solution.py:28
  198.9 4.9 %fusion.256 = bf16[3,384,384]{1,2,0:T(8,128)(2,1)} fusion(bf16[3,384,384]{1,2,0:T(8,128)(2,1)} %get-tuple-element.367, s32[]{:T(128)} %get-tuple-element.366, f32[384,384]{1,0:T(8,128)} %fusion.254, f32[384,384]{1,0:T(8,128)} %fusion.255, bf16[384,384]{1,0:T(8,128)(2,1)S(1)} %fusion.253, f32[384]{0:T(512)S(1)} %get-tuple-element.351, ...), kind=kOutput, calls=%fused_computation.19.clone.1 | convolution fusion | flops 230473728 | bytes 1773057 | tf_op jit(solution)/shard_map/while/body/eval_jaxpr/dot_general | solution.py:28
  220.7 4.6 %add_bitcast_fusion.3 = f32[5,384,384]{1,2,0:T(8,128)} fusion(f32[5,384,384]{2,1,0:T(8,128)S(1)} %fusion.243, bf16[5,384,384]{2,1,0:T(8,128)(2,1)S(1)} %negate_convert_fusion.2), kind=kOutput, calls=%fused_computation.5.clone.1 | convolution fusion | flops 568442880 | bytes 7372800 | tf_op jit(solution)/shard_map/while/body/eval_jaxpr/jk,pkl->pjl/dot_general | solution.py:24
  225.3 5.7 %copy.132 = f32[5,384,384]{2,0,1:T(8,128)} copy(f32[5,384,384]{1,2,0:T(8,128)} %add_bitcast_fusion.3) | data formatting | bytes 5898240 | tf_op jit(solution)/shard_map/while/body/eval_jaxpr/add | solution.py:70
  232.3 8.8 %fusion.249 = f32[5,384,384]{2,0,1:T(8,128)} fusion(f32[5,384,384]{2,0,1:T(8,128)} %copy.132, f32[5]{0:T(128)S(1)} %multiply_add_fusion.2, f32[5]{0:T(128)S(1)} %add_convert_fusion.2), kind=kOutput, calls=%fused_computation.121.clone.1 | convolution fusion | flops 44236848 | bytes 5898280 | tf_op jit(solution)/shard_map/while/body/eval_jaxpr/mp,pxy->mxy/dot_general | solution.py:32
  248.7 5.4 %copy.131 = f32[5,384,384]{2,0,1:T(8,128)} copy(f32[5,384,384]{1,2,0:T(8,128)} %subtract_bitcast_fusion.2) | data formatting | bytes 5898240 | tf_op jit(solution)/shard_map/while/body/eval_jaxpr/sub | solution.py:73
  254.0 6.3 %fusion.250 = f32[5,384,384]{2,0,1:T(8,128)S(1)} fusion(f32[5,384,384]{2,0,1:T(8,128)} %copy.131, f32[5]{0:T(128)S(1)} %multiply_add_fusion.2, f32[5]{0:T(128)S(1)} %add_convert_fusion.2), kind=kOutput, calls=%fused_computation.117.clone.1 | convolution fusion | flops 44236848 | bytes 5898280 | tf_op jit(solution)/shard_map/while/body/eval_jaxpr/mp,pxy->mxy/dot_general | solution.py:32
  264.3 5.0 %fusion.244 = f32[5,384,384]{2,0,1:T(8,128)S(1)} fusion(f32[5,384,384]{2,0,1:T(8,128)S(1)} %bitcast.249, f32[5]{0:T(128)S(1)} %multiply_add_fusion.2, f32[5]{0:T(128)S(1)} %add_convert_fusion.2), kind=kOutput, calls=%fused_computation.118.clone.1 | convolution fusion | flops 44236848 | bytes 5898280 | tf_op jit(solution)/shard_map/while/body/eval_jaxpr/mp,pxy->mxy/dot_general | solution.py:32
  269.3 5.0 %fusion.242 = f32[5,384,384]{2,0,1:T(8,128)S(1)} fusion(f32[5,384,384]{2,0,1:T(8,128)S(1)} %bitcast.251, f32[5]{0:T(128)S(1)} %multiply_add_fusion.2, f32[5]{0:T(128)S(1)} %add_convert_fusion.2), kind=kOutput, calls=%fused_computation.122.clone.1 | convolution fusion | flops 44236848 | bytes 5898280 | tf_op jit(solution)/shard_map/while/body/eval_jaxpr/mp,pxy->mxy/dot_general | solution.py:32
  281.1 4.8 %fusion.254 = f32[384,384]{1,0:T(8,128)} fusion(f32[384,384]{1,0:T(8,128)} %fusion.248, bf16[384,384]{1,0:T(8,128)(2,1)S(1)} %fusion.253), kind=kOutput, calls=%fused_computation.20.clone.1 | convolution fusion | flops 229736448 | bytes 1474560 | tf_op jit(solution)/shard_map/while/body/eval_jaxpr/dot_general | solution.py:28
  294.3 4.9 %fusion.256 = bf16[3,384,384]{1,2,0:T(8,128)(2,1)} fusion(bf16[3,384,384]{1,2,0:T(8,128)(2,1)} %get-tuple-element.367, s32[]{:T(128)} %get-tuple-element.366, f32[384,384]{1,0:T(8,128)} %fusion.254, f32[384,384]{1,0:T(8,128)} %fusion.255, bf16[384,384]{1,0:T(8,128)(2,1)S(1)} %fusion.253, f32[384]{0:T(512)S(1)} %get-tuple-element.351, ...), kind=kOutput, calls=%fused_computation.19.clone.1 | convolution fusion | flops 230473728 | bytes 1773057 | tf_op jit(solution)/shard_map/while/body/eval_jaxpr/dot_general | solution.py:28
  313.9 28.5 %all-to-all-done.1 = bf16[8,384,384]{2,1,0:T(8,128)(2,1)S(1)} async-done(((bf16[8,384,384]{2,1,0:T(8,128)(2,1)}), bf16[8,384,384]{2,1,0:T(8,128)(2,1)S(1)}, u32[]{:S(2)}, u32[]{:S(2)}) %all-to-all-start.1) | async-done | bytes 2359328 | tf_op jit(solution)/shard_map/all_to_all | solution.py:175
  350.0 5.0 %collective-permute-done.1 = bf16[320,64]{1,0:T(8,128)(2,1)S(1)} collective-permute-done((bf16[320,64]{1,0:T(8,128)(2,1)S(1)}, bf16[320,64]{1,0:T(8,128)(2,1)S(1)}, u32[]{:S(2)}, u32[]{:S(2)}) %collective-permute-start.1) | collective-permute-done | bytes 40992 | tf_op jit(solution)/shard_map/ppermute | solution.py:20
  (232 shorter events, 144.8 us)
Async XLA Ops:
  0.0 10.1 %copy-start.4 = (f32[384,384]{1,0:T(8,128)S(1)}, f32[384,384]{1,0:T(8,128)}, u32[]{:S(2)}) copy-start(f32[384,384]{1,0:T(8,128)} %param.12) | copy-start | bytes 1769476
  2.6 306.2 %all-to-all-start = ((s32[8,1,1]{2,1,0:T(1,128)}), s32[8,1,1]{2,1,0:T(1,128)}, u32[]{:S(2)}, u32[]{:S(2)}) async-start(s32[8,1,1]{2,1,0:T(1,128)} %copy.99), calls=%async_computation | async-start | bytes 8192 | tf_op jit(solution)/shard_map/all_to_all | solution.py:176
  13.1 292.6 %copy-start.9 = (s32[3]{0:T(128)S(1)}, s32[3]{0:T(128)}, u32[]{:S(2)}) copy-start(s32[3]{0:T(128)} %copy-done.8) | copy-start | bytes 40
  13.2 292.6 %copy-start.11 = (pred[3]{0:T(512)(128)(4,1)S(1)}, pred[3]{0:T(512)(128)(4,1)}, u32[]{:S(2)}) copy-start(pred[3]{0:T(512)(128)(4,1)} %copy-done.10) | copy-start | bytes 13
  21.5 7.3 %copy-start = (bf16[5,384,384]{2,1,0:T(8,128)(2,1)}, bf16[5,384,384]{2,1,0:T(8,128)(2,1)S(1)}, u32[]{:S(2)}) copy-start(bf16[5,384,384]{2,1,0:T(8,128)(2,1)S(1)} %convolution_convert_fusion.3) | copy-start | bytes 4423684 | tf_op jit(solution)/shard_map/while
  41.7 8.8 %copy-start.3 = (bf16[5,384,384]{2,1,0:T(8,128)(2,1)S(1)}, bf16[5,384,384]{2,1,0:T(8,128)(2,1)}, u32[]{:S(2)}) copy-start(bf16[5,384,384]{2,1,0:T(8,128)(2,1)} %copy-done.2) | copy-start | bytes 4423684 | tf_op jit(solution)/shard_map/while
  50.5 3.0 copy-start.1
  58.1 11.7 %slice-start.4 = ((s8[4718592]{0:T(1024)(128)(4,1)}), s8[524288]{0:T(1024)(128)(4,1)S(1)}, s32[]{:S(2)}) async-start(s8[4718592]{0:T(1024)(128)(4,1)} %bitcast.252), calls=%async_computation.6 | async-start | bytes 1048576 | tf_op jit(solution)/shard_map/while
  63.5 6.4 %slice-start.5 = ((s8[4718592]{0:T(1024)(128)(4,1)}), s8[4194304]{0:T(1024)(128)(4,1)S(1)}, s32[]{:S(2)}) async-start(s8[4718592]{0:T(1024)(128)(4,1)} %bitcast.252), calls=%async_computation.7 | async-start | bytes 8388608 | tf_op jit(solution)/shard_map/while
  71.4 2.2 slice-start
  71.6 2.2 slice-start.1
  71.6 7.1 %slice-start.2 = ((s8[4718592]{0:T(1024)(128)(4,1)}), s8[4194304]{0:T(1024)(128)(4,1)S(1)}, s32[]{:S(2)}) async-start(s8[4718592]{0:T(1024)(128)(4,1)} %bitcast.250), calls=%async_computation.4 | async-start | bytes 8388608 | tf_op jit(solution)/shard_map/while
  73.8 5.0 %slice-start.3 = ((s8[4718592]{0:T(1024)(128)(4,1)}), s8[524288]{0:T(1024)(128)(4,1)S(1)}, s32[]{:S(2)}) async-start(s8[4718592]{0:T(1024)(128)(4,1)} %bitcast.250), calls=%async_computation.5 | async-start | bytes 1048576 | tf_op jit(solution)/shard_map/while
  117.0 7.3 %copy-start = (bf16[5,384,384]{2,1,0:T(8,128)(2,1)}, bf16[5,384,384]{2,1,0:T(8,128)(2,1)S(1)}, u32[]{:S(2)}) copy-start(bf16[5,384,384]{2,1,0:T(8,128)(2,1)S(1)} %convolution_convert_fusion.3) | copy-start | bytes 4423684 | tf_op jit(solution)/shard_map/while
  136.9 8.8 %copy-start.3 = (bf16[5,384,384]{2,1,0:T(8,128)(2,1)S(1)}, bf16[5,384,384]{2,1,0:T(8,128)(2,1)}, u32[]{:S(2)}) copy-start(bf16[5,384,384]{2,1,0:T(8,128)(2,1)} %copy-done.2) | copy-start | bytes 4423684 | tf_op jit(solution)/shard_map/while
  145.7 3.0 copy-start.1
  153.3 11.9 %slice-start.4 = ((s8[4718592]{0:T(1024)(128)(4,1)}), s8[524288]{0:T(1024)(128)(4,1)S(1)}, s32[]{:S(2)}) async-start(s8[4718592]{0:T(1024)(128)(4,1)} %bitcast.252), calls=%async_computation.6 | async-start | bytes 1048576 | tf_op jit(solution)/shard_map/while
  158.6 6.6 %slice-start.5 = ((s8[4718592]{0:T(1024)(128)(4,1)}), s8[4194304]{0:T(1024)(128)(4,1)S(1)}, s32[]{:S(2)}) async-start(s8[4718592]{0:T(1024)(128)(4,1)} %bitcast.252), calls=%async_computation.7 | async-start | bytes 8388608 | tf_op jit(solution)/shard_map/while
  166.8 2.2 slice-start
  167.0 7.1 %slice-start.2 = ((s8[4718592]{0:T(1024)(128)(4,1)}), s8[4194304]{0:T(1024)(128)(4,1)S(1)}, s32[]{:S(2)}) async-start(s8[4718592]{0:T(1024)(128)(4,1)} %bitcast.250), calls=%async_computation.4 | async-start | bytes 8388608 | tf_op jit(solution)/shard_map/while
  169.1 5.0 %slice-start.3 = ((s8[4718592]{0:T(1024)(128)(4,1)}), s8[524288]{0:T(1024)(128)(4,1)S(1)}, s32[]{:S(2)}) async-start(s8[4718592]{0:T(1024)(128)(4,1)} %bitcast.250), calls=%async_computation.5 | async-start | bytes 1048576 | tf_op jit(solution)/shard_map/while
  212.2 7.3 %copy-start = (bf16[5,384,384]{2,1,0:T(8,128)(2,1)}, bf16[5,384,384]{2,1,0:T(8,128)(2,1)S(1)}, u32[]{:S(2)}) copy-start(bf16[5,384,384]{2,1,0:T(8,128)(2,1)S(1)} %convolution_convert_fusion.3) | copy-start | bytes 4423684 | tf_op jit(solution)/shard_map/while
  232.3 8.8 %copy-start.3 = (bf16[5,384,384]{2,1,0:T(8,128)(2,1)S(1)}, bf16[5,384,384]{2,1,0:T(8,128)(2,1)}, u32[]{:S(2)}) copy-start(bf16[5,384,384]{2,1,0:T(8,128)(2,1)} %copy-done.2) | copy-start | bytes 4423684 | tf_op jit(solution)/shard_map/while
  241.1 3.0 copy-start.1
  248.7 11.7 %slice-start.4 = ((s8[4718592]{0:T(1024)(128)(4,1)}), s8[524288]{0:T(1024)(128)(4,1)S(1)}, s32[]{:S(2)}) async-start(s8[4718592]{0:T(1024)(128)(4,1)} %bitcast.252), calls=%async_computation.6 | async-start | bytes 1048576 | tf_op jit(solution)/shard_map/while
  254.0 6.4 %slice-start.5 = ((s8[4718592]{0:T(1024)(128)(4,1)}), s8[4194304]{0:T(1024)(128)(4,1)S(1)}, s32[]{:S(2)}) async-start(s8[4718592]{0:T(1024)(128)(4,1)} %bitcast.252), calls=%async_computation.7 | async-start | bytes 8388608 | tf_op jit(solution)/shard_map/while
  262.0 2.2 slice-start
  262.2 7.1 %slice-start.2 = ((s8[4718592]{0:T(1024)(128)(4,1)}), s8[4194304]{0:T(1024)(128)(4,1)S(1)}, s32[]{:S(2)}) async-start(s8[4718592]{0:T(1024)(128)(4,1)} %bitcast.250), calls=%async_computation.4 | async-start | bytes 8388608 | tf_op jit(solution)/shard_map/while
  264.3 5.0 %slice-start.3 = ((s8[4718592]{0:T(1024)(128)(4,1)}), s8[524288]{0:T(1024)(128)(4,1)S(1)}, s32[]{:S(2)}) async-start(s8[4718592]{0:T(1024)(128)(4,1)} %bitcast.250), calls=%async_computation.5 | async-start | bytes 1048576 | tf_op jit(solution)/shard_map/while
  308.8 33.6 %all-to-all-start.1 = ((bf16[8,384,384]{2,1,0:T(8,128)(2,1)}), bf16[8,384,384]{2,1,0:T(8,128)(2,1)S(1)}, u32[]{:S(2)}, u32[]{:S(2)}) async-start(bf16[8,384,384]{2,1,0:T(8,128)(2,1)} %copy.101), calls=%async_computation.1 | async-start | bytes 4718592 | tf_op jit(solution)/shard_map/all_to_all | solution.py:175
  345.1 3.2 collective-permute-start
  348.4 6.5 %collective-permute-start.1 = (bf16[320,64]{1,0:T(8,128)(2,1)S(1)}, bf16[320,64]{1,0:T(8,128)(2,1)S(1)}, u32[]{:S(2)}, u32[]{:S(2)}) collective-permute-start(bf16[320,64]{1,0:T(8,128)(2,1)S(1)} %fusion.150), channel_id=1, source_target_pairs={{8,0},{16,8},{24,16},{9,1},{17,9},{25,17},{10,2},{18,10},{26,18},{... | collective-permute-start | bytes 122888 | tf_op jit(solution)/shard_map/ppermute | solution.py:20
  (14 other events, 14.4 us)
where the time goes:
time: 360 us; the launch traced here: 356 us
  matrix products  202 us (56%)
  local copies, waits for them, and re-layouts  69.6 us (19%)
  waiting for transfers between devices  35.2 us (10%)
  other arithmetic  21.4 us (6%)
  loops' own time  16.1 us (4%)
  starting transfers between devices  12 us (3%)
    dot_general x12, matrix products, mix_bands(): jnp.einsum(pattern, operand_a, operand_b, precision=lax.Precision.HIGHEST)  75.5 us
    dot_general x20, matrix products, batched(): jnp.einsum(pattern, operand_a, operand_b, preferred_element_type=jnp.floa...  74.4 us
    dot_general x12, matrix products, plain_dot(): return jnp.dot(operand_a, operand_b, preferred_element_type=jnp.float32)  51.6 us
    all_to_all x1, waiting for transfers between devices, shards(): lax.all_to_all(outgoing, 'ty', split_axis=0, concat_axis=0, tiled=True)  28.5 us
    add x3, local copies, waits for them, and re-layouts, tile_image(): batched('jk,pkl->pjl', cosine, first_real)  16.9 us
    another operation x1, loops' own time, shards(): results = lax.map(one_slot, (frames[0], masks[0], phases[0], own_tiles))  16.1 us
    sub x3, local copies, waits for them, and re-layouts, tile_image(): batched('jk,pkl->pjl', cosine, first_imag)  16.1 us
    mul x6, local copies, waits for them, and re-layouts, tile_image(): shaped * cell_mask.astype(jnp.bfloat16)[None, :, None, :, None]  11.3 us
  transfers between devices with their start and end apart: 4, of which 3 were waited for; matrix products, arithmetic and copies ran while one was open for 77% of the time, Pallas kernels for 0%

commit v1 on v0

v1 whole, which is shorter than its diff:
```python
import math

import jax
import jax.numpy as jnp
import numpy as np
from jax import lax
from jax.experimental import pallas as pl
from jax.experimental.pallas import tpu as pltpu
from jax.sharding import PartitionSpec as P

STRIDE = 320
GROUP_COLS = 2


wiener = 0.1
pattern_base = (37, 101)
pattern_step = (29, -53)


def passed_along(value, axis, steps):
    count = lax.axis_size(axis)
    leading, last = (max(0, -steps), min(count, count - steps))
    return lax.ppermute(value, axis, [(source, source + steps) for source in range(leading, last)])


def batched(pattern, operand_a, operand_b):
    return jnp.einsum(pattern, operand_a, operand_b, preferred_element_type=jnp.float32)


def pattern_shift(orient):
    return (pattern_base[0] + orient * pattern_step[0], pattern_base[1] + orient * pattern_step[1])


def tables(length, halfway):
    places = np.arange(length)
    angles = (places[:, None] * places[None, :] % length) * (2.0 * math.pi / length)
    cosine, sine = (np.cos(angles), np.sin(angles))
    rows, cols = pattern_shift(0)
    right, left = [], []
    for m in range(halfway + 1):
        right.append(np.concatenate([np.roll(cosine, -m * cols, 1), -np.roll(sine, -m * cols, 1)], 1))
        left.append(np.concatenate([np.roll(cosine, -m * rows, 0), np.roll(sine, -m * rows, 0)], 1))
    return (
        jnp.asarray(np.stack(right).astype(jnp.bfloat16)),
        jnp.asarray(np.stack(left).astype(jnp.bfloat16)),
    )


def dot(a, b):
    return jnp.dot(a, b, preferred_element_type=jnp.float32)


def tile_kernel(
    phase_count, cells, intersection,
    coef_ref, flags_ref, frames_ref, mask_ref, right_ref, left_ref, otf_ref, apod_ref,
    out_ref,
    wide_ref, gain_ref, images_ref, waves_ref, spec_ref, mid_ref,
):
    step = pl.program_id(0)
    length = otf_ref.shape[-1]
    halfway = phase_count // 2
    shift_rows, shift_cols = pattern_shift(0)
    chunk = length // 3

    @pl.when(step == 0)
    def _():
        for m in range(1, halfway + 1):
            c, neg_s = (right_ref[m, :, :length], right_ref[m, :, length:])
            wide_ref[m, :length, :length] = c
            wide_ref[m, :length, length:] = neg_s
            wide_ref[m, length:, :length] = -neg_s
            wide_ref[m, length:, length:] = c
        c, neg_s = (right_ref[0, :, :length], right_ref[0, :, length:])
        wide_ref[0, :length, :length] = c
        wide_ref[0, :length, length:] = -neg_s
        wide_ref[0, length:, :length] = neg_s
        wide_ref[0, length:, length:] = c

        for side in range(2):
            def rolled(m):
                value = otf_ref[side]
                if m == 0:
                    return value
                value = pltpu.roll(value, (-m * shift_rows) % length, 0)
                return pltpu.roll(value, (-m * shift_cols) % length, 1)

            total = jnp.full((length, length), wiener, jnp.float32)
            for m in range(-halfway, halfway + 1):
                value = rolled(m)
                total = total + value * value
                if side == 0 and m >= 0:
                    gain_ref[m] = value
                if side == 1 and m > 0:
                    spec_side = value
                    mid_slot = halfway + m
                    gain_ref[mid_slot] = spec_side
            scale = apod_ref[side] / total
            if side == 0:
                for m in range(halfway + 1):
                    gain_ref[m] = gain_ref[m] * scale
            else:
                for m in range(1, halfway + 1):
                    gain_ref[m] = gain_ref[m] + gain_ref[halfway + m] * scale

    width = length // cells
    for cell in range(cells):
        rows = pl.ds(cell * width, width)
        keep = mask_ref[0, cell:cell + 1, :].astype(jnp.float32)
        planes = [frames_ref[0, 0, 0, p, rows, :].astype(jnp.float32) * keep for p in range(phase_count)]
        total = planes[0]
        for p in range(1, phase_count):
            total = total + planes[p]
        images_ref[0, rows, :length] = (total * (1.0 / phase_count)).astype(jnp.bfloat16)
        for m in range(1, halfway + 1):
            for part in range(2):
                base = ((step * (halfway + 1) + m) * 2 + part) * phase_count
                total = planes[0] * coef_ref[base]
                for p in range(1, phase_count):
                    total = total + planes[p] * coef_ref[base + p]
                images_ref[m, rows, part * length:(part + 1) * length] = total.astype(jnp.bfloat16)

    for m in range(halfway + 1):
        for third in range(3):
            rows = pl.ds(third * chunk, chunk)
            lower = pl.ds(length + third * chunk, chunk)
            if m == 0:
                wave = dot(images_ref[0, rows, :length], right_ref[0])
            else:
                wave = dot(images_ref[m, rows, :], wide_ref[m])
            wave = wave.astype(jnp.bfloat16)
            waves_ref[m, rows, :] = wave
            waves_ref[m, lower, :length] = wave[:, length:]
            waves_ref[m, lower, length:] = -wave[:, :length]

    for third in range(3):
        rows = pl.ds(third * chunk, chunk)
        total = None
        for m in range(halfway + 1):
            band = dot(left_ref[m, rows, :], waves_ref[m])
            gain = gain_ref[m, rows, :]
            term = jnp.concatenate([gain, gain], axis=1) * band
            total = term if total is None else total + term
        spec_ref[rows, :] = total.astype(jnp.bfloat16)

    for third in range(3):
        rows = pl.ds(third * chunk, chunk)
        mid = dot(spec_ref[rows, :], wide_ref[0]).astype(jnp.bfloat16)
        mid_ref[rows, :] = mid[:, :length]
        mid_ref[pl.ds(length + third * chunk, chunk), :] = mid[:, length:]

    held = flags_ref[step * 3] > 0
    row_last = flags_ref[step * 3 + 1] > 0
    column_last = flags_ref[step * 3 + 2] > 0

    def ramp(places, is_last):
        places = places.astype(jnp.float32) + 0.5
        rising = jnp.minimum(places / intersection, 1.0)
        falling = jnp.minimum((length - places) / intersection, 1.0)
        return rising * jnp.where(is_last, jnp.ones_like(falling), falling)

    for third in range(3):
        rows = pl.ds(third * chunk, chunk)
        picture = dot(right_ref[0, rows, :], mid_ref[...]) * (1.0 / (length * length))
        places = lax.broadcasted_iota(jnp.int32, (chunk, length), 0) + third * chunk
        picture = picture * ramp(places, row_last)
        picture = picture * ramp(lax.broadcasted_iota(jnp.int32, (chunk, length), 1), column_last)
        out_ref[0, rows, :] = jnp.where(held, picture, 0.0).astype(jnp.bfloat16)


def reversed_map(value):
    return jnp.roll(value[::-1, ::-1], (1, 1), (0, 1))


def tile_results(frames, masks, phases, own_tiles, otf, apod, row_last, column_last, intersection):
    slot_count, phase_count = (frames.shape[1], frames.shape[3])
    length = otf.shape[0]
    cells = masks.shape[-1]
    halfway = phase_count // 2
    orders = jnp.arange(0, halfway + 1).astype(jnp.float32)
    phase_steps = jnp.arange(phase_count).astype(jnp.float32) * (2.0 * math.pi / phase_count)
    angles = orders[None, :, None] * (phases[0] + phase_steps[None, :])[:, None, :]
    coef = jnp.stack([jnp.cos(angles), -jnp.sin(angles)], axis=2) / phase_count
    flags = jnp.stack([own_tiles >= 0, row_last, column_last], axis=1).astype(jnp.int32)
    mask_rows = jnp.repeat(masks[0].astype(jnp.bfloat16), length // cells, axis=2)
    right, left = tables(length, halfway)
    otfs = jnp.stack([otf, reversed_map(otf)])
    apods = jnp.stack([apod, reversed_map(apod)])
    bands = halfway + 1

    def whole(array):
        return pl.BlockSpec(array.shape, lambda s: (0,) * array.ndim)

    return pl.pallas_call(
        lambda *refs: tile_kernel(phase_count, cells, intersection, *refs),
        grid=(slot_count,),
        in_specs=[
            pl.BlockSpec(memory_space=pltpu.SMEM),
            pl.BlockSpec(memory_space=pltpu.SMEM),
            pl.BlockSpec((1, 1) + frames.shape[2:], lambda s: (0, s, 0, 0, 0, 0)),
            pl.BlockSpec((1, cells, length), lambda s: (s, 0, 0)),
            whole(right), whole(left), whole(otfs), whole(apods),
        ],
        out_specs=pl.BlockSpec((1, length, length), lambda s: (s, 0, 0)),
        out_shape=jax.ShapeDtypeStruct((slot_count, length, length), jnp.bfloat16),
        scratch_shapes=[
            pltpu.VMEM((bands, 2 * length, 2 * length), jnp.bfloat16),
            pltpu.VMEM((2 * halfway + 1, length, length), jnp.float32),
            pltpu.VMEM((bands, length, 2 * length), jnp.bfloat16),
            pltpu.VMEM((bands, 2 * length, 2 * length), jnp.bfloat16),
            pltpu.VMEM((length, 2 * length), jnp.bfloat16),
            pltpu.VMEM((2 * length, length), jnp.bfloat16),
        ],
        compiler_params=pltpu.CompilerParams(vmem_limit_bytes=60 * 1024 * 1024),
    )(coef.reshape(-1), flags.reshape(-1), frames, mask_rows, right, left, otfs, apods)


def fold_rows(padded_block, intersection):
    arrived = passed_along(padded_block[:intersection].astype(jnp.bfloat16), "ty", -1).astype(
        jnp.float32
    )
    interior = padded_block[intersection:]
    keep_rows = interior.shape[0] - intersection
    return jnp.concatenate([interior[:keep_rows], interior[keep_rows:] + arrived], axis=0)


def fold_columns(padded_block, intersection):
    arrived = passed_along(padded_block[:, :intersection].astype(jnp.bfloat16), "tx", -1).astype(
        jnp.float32
    )
    interior = padded_block[:, intersection:]
    keep_cols = interior.shape[1] - intersection
    return jnp.concatenate([interior[:, :keep_cols], interior[:, keep_cols:] + arrived], axis=1)


def shards(frames, masks, phases, slot_tile, otf, apod):
    row_count = lax.axis_size("ty")
    group_count = lax.axis_size("tx")
    my_group = lax.axis_index("tx")
    length = otf.shape[0]
    intersection = length - STRIDE
    own_tiles = slot_tile[0]

    tile_rows = own_tiles // GROUP_COLS
    columns = GROUP_COLS * my_group + own_tiles % GROUP_COLS
    results = tile_results(
        frames, masks, phases, own_tiles, otf, apod,
        tile_rows == row_count - 1, columns == GROUP_COLS * group_count - 1, intersection,
    )
    column_places = jnp.arange(GROUP_COLS, dtype=jnp.int32)
    owner_rows = jnp.arange(row_count, dtype=jnp.int32)
    matches = ((own_tiles // GROUP_COLS)[:, None] == owner_rows[None, :]) & (own_tiles >= 0)[
        :, None
    ]
    choose = matches.astype(jnp.bfloat16)
    outgoing = batched("sh,sxy->hxy", choose, results).astype(jnp.bfloat16)
    labels = jnp.sum(matches.astype(jnp.int32) * (own_tiles % GROUP_COLS + 1)[:, None], axis=0) - 1
    incoming, column_tags = (
        lax.all_to_all(outgoing, "ty", split_axis=0, concat_axis=0, tiled=True),
        lax.all_to_all(labels[:, None], "ty", split_axis=0, concat_axis=0, tiled=True),
    )
    selector = (column_tags == column_places[None, :]).astype(jnp.bfloat16)
    tiles_here = batched("sc,sxy->cxy", selector, incoming)
    padded = jnp.zeros((length, STRIDE * GROUP_COLS + intersection), jnp.float32)
    for column_place in range(GROUP_COLS):
        padded = padded + jnp.pad(
            tiles_here[column_place],
            ((0, 0), (STRIDE * column_place, STRIDE * (GROUP_COLS - 1 - column_place))),
        )
    stitched = fold_columns(fold_rows(padded, intersection), intersection)
    return stitched


def solution(mesh):
    in_specs = (
        P("tx", "ty", None, None, None, None),
        P("tx", "ty", None, None),
        P("tx", "ty", None),
        P("tx", "ty"),
        P(),
        P(),
    )
    out_specs = P("ty", "tx")
    return jax.shard_map(shards, mesh=mesh, in_specs=in_specs, out_specs=out_specs, check_vma=False)
```

time: 360 us -> 89.6 us (0.25)
  matrix products: 202 us -> 5.97 us
  local copies, waits for them, and re-layouts: 69.6 us -> 11 us
  Pallas kernels: 0 us -> 18.3 us
  loops' own time: 16.1 us -> 0 us
  other arithmetic: 21.4 us -> 5.9 us
    dot_general x24 -> x0, matrix products: 127 us -> none  [the longest x12 75.5 us: mix_bands(): jnp.einsum(pattern, operand_a, operand_b, precision=lax.Precision.HIGHEST)]
    dot_general x20 -> x2, matrix products: 74.4 us -> 5.97 us  [batched(): jnp.einsum(pattern, operand_a, operand_b, preferred_element_type=jnp.floa...]
    pallas_call x0 -> x1, Pallas kernels: none -> 18.3 us  [tile_results(): pl.pallas_call(lambda *refs: tile_kernel(phase_count, cells, intersection...]
    add x3 -> x0, local copies, waits for them, and re-layouts: 16.9 us -> none  [tile_image(): batched('jk,pkl->pjl', cosine, first_real)]
    another operation x1 -> x0, loops' own time: 16.1 us -> none  [shards(): results = lax.map(one_slot, (frames[0], masks[0], phases[0], own_tiles))]
    sub x3 -> x0, local copies, waits for them, and re-layouts: 16.1 us -> none  [tile_image(): batched('jk,pkl->pjl', cosine, first_imag)]
    while x67 -> x0, local copies, waits for them, and re-layouts: 12.4 us -> none
    mul x6 -> x0, local copies, waits for them, and re-layouts: 11.3 us -> none  [tile_image(): shaped * cell_mask.astype(jnp.bfloat16)[None, :, None, :, None]]
  transfers between devices with their start and end apart: 4 -> 4, of which waited for: 3 -> 3; matrix products, arithmetic and copies ran while one was open for 77% -> 18% of each run, Pallas kernels for 0% -> 20%
where the time goes in v1:
time: 89.6 us; the launch traced here: 89.2 us
  waiting for transfers between devices  35.8 us (40%)
  Pallas kernels  18.3 us (20%)
  starting transfers between devices  12 us (13%)
  local copies, waits for them, and re-layouts  11 us (12%)
  matrix products  5.97 us (7%)
  other arithmetic  5.9 us (7%)
    all_to_all x1, waiting for transfers between devices, shards(): lax.all_to_all(outgoing, 'ty', split_axis=0, concat_axis=0, tiled=True)  29.2 us
    pallas_call x1, Pallas kernels, tile_results(): pl.pallas_call(lambda *refs: tile_kernel(phase_count, cells, intersection...  18.3 us
    ppermute x2, waiting for transfers between devices, passed_along(): lax.ppermute(value, axis, [(source, source + steps) for source in range(l...  6.65 us
    dot_general x2, matrix products, batched(): jnp.einsum(pattern, operand_a, operand_b, preferred_element_type=jnp.floa...  5.97 us
    all_to_all x1, starting transfers between devices, shards(): lax.all_to_all(labels[:, None], 'ty', split_axis=0, concat_axis=0, tiled=...  5.2 us
    slice x10, local copies, waits for them, and re-layouts, reversed_map(): return jnp.roll(value[::-1, ::-1], (1, 1), (0, 1))  4.77 us
    all_to_all x1, starting transfers between devices, shards(): lax.all_to_all(outgoing, 'ty', split_axis=0, concat_axis=0, tiled=True)  4.19 us
    ppermute x2, starting transfers between devices, passed_along(): lax.ppermute(value, axis, [(source, source + steps) for source in range(l...  2.58 us
  transfers between devices with their start and end apart: 4, of which 3 were waited for; matrix products, arithmetic and copies ran while one was open for 18% of the time, Pallas kernels for 20%

profile of v1, /device:TPU:0, one launch (start us, length us, event | category | flops | bytes accessed | tf_op | source)
XLA Modules:
  0.0 89.2 jit_solution(8977557801366229107)
XLA Ops:
  0.0 0.7 bitcast_compare_fusion.1
  0.7 0.7 fusion.24
  1.5 0.7 copy.15
  2.2 5.2 %all-to-all-start = ((s32[8,1,1]{2,1,0:T(1,128)}), s32[8,1,1]{2,1,0:T(1,128)S(1)}, u32[]{:S(2)}, u32[]{:S(2)}) async-start(s32[8,1,1]{2,1,0:T(1,128)} %copy.15), calls=%async_computation | async-start | bytes 8192 | tf_op jit(solution)/shard_map/all_to_all | solution.py:259
  7.4 1.1 %slice.74 = f32[383,384]{1,0:T(8,128)S(1)} slice(f32[384,384]{1,0:T(8,128)} %param.12), slice={[1:384], [0:384]} | slice | bytes 1176576 | tf_op jit(solution)/shard_map/jit(_roll_static)/slice | solution.py:171
  8.8 0.6 reshape.212.refs_1_
  9.4 0.3 slice.73
  9.7 0.3 slice.79
  10.0 0.2 multiply_cosine_fusion
  10.3 0.7 div.31.refs_0_
  11.1 0.8 reshape.211.refs_3_
  11.9 1.5 %slice.75 = f32[383,384]{1,0:T(8,128)S(1)} reverse(f32[383,384]{1,0:T(8,128)S(1)} %slice.74), dimensions={0,1} | reverse | bytes 1176576 | tf_op jit(solution)/shard_map/jit(_roll_static)/slice | solution.py:171
  13.4 1.5 %slice.81 = f32[383,384]{1,0:T(8,128)S(1)} reverse(f32[383,384]{1,0:T(8,128)S(1)} %slice.80), dimensions={0,1} | reverse | bytes 1176576 | tf_op jit(solution)/shard_map/jit(_roll_static)/slice | solution.py:171
  15.0 0.3 fusion.8
  15.2 0.3 fusion.6
  15.5 0.5 copy-done
  16.0 1.6 %pad_maximum_fusion = (f32[2,384,384]{2,1,0:T(8,128)}, f32[2,384,384]{2,1,0:T(8,128)}) fusion(f32[1,384,384]{2,1,0:T(8,128)S(1)} %fusion.8, f32[1,384,384]{2,1,0:T(8,128)S(1)} %bitcast.64, f32[1,384,384]{2,1,0:T(8,128)S(1)} %fusion.6, f32[1,384,384]{2,1,0:T(8,128)S(1)} %bitcast.65), kind=kLoop, calls=%fused_computation.9 | loop fusion | flops 589824 | bytes 4718592 | tf_op jit(solution)/shard_map/stack | solution.py:186
  17.6 18.3 %shard_map.82 = bf16[3,384,384]{2,1,0:T(8,128)(2,1)} custom-call(f32[90]{0:T(128)} %div.31.refs_0_, s32[9]{0:T(128)} %reshape.212.refs_1_, bf16[1,3,1,5,384,384]{5,4,3,2,1,0:T(8,128)(2,1)} %refs_2_.1, bf16[3,12,384]{2,1,0:T(8,128)(2,1)} %reshape.211.refs_3_, bf16[3,384,768]{2,1,0:T(8,128)(2,1)} %constant.55.clone.refs_4_, ...), custom_call_target="tpu_custom_call" | custom-call | tf_op jit(solution)/shard_map/pallas_call | solution.py:193
  35.8 4.4 %convolution_convert_fusion = bf16[8,384,384]{2,0,1:T(8,128)(2,1)S(1)} fusion(bf16[3,384,384]{2,1,0:T(8,128)(2,1)} %shard_map.82, s32[3]{0:T(128)S(1)} %get-tuple-element.10, pred[3]{0:T(512)(128)(4,1)S(1)} %bitcast_compare_fusion.1), kind=kOutput, calls=%fused_computation.2 | convolution fusion | flops 8257584 | bytes 3244047 | tf_op jit(solution)/shard_map/sh,sxy->hxy/dot_general | solution.py:27
  40.2 1.7 %copy.18 = bf16[8,384,384]{2,1,0:T(8,128)(2,1)} copy(bf16[8,384,384]{2,0,1:T(8,128)(2,1)S(1)} %convolution_convert_fusion) | data formatting | bytes 4718592 | tf_op jit(solution)/shard_map/convert_element_type | solution.py:255
  42.0 4.2 %all-to-all-start.1 = ((bf16[8,384,384]{2,1,0:T(8,128)(2,1)}), bf16[8,384,384]{2,1,0:T(8,128)(2,1)S(1)}, u32[]{:S(2)}, u32[]{:S(2)}) async-start(bf16[8,384,384]{2,1,0:T(8,128)(2,1)} %copy.18), calls=%async_computation.1 | async-start | bytes 4718592 | tf_op jit(solution)/shard_map/all_to_all | solution.py:258
  46.2 0.2 reduce
  46.4 29.2 %all-to-all-done.1 = bf16[8,384,384]{2,1,0:T(8,128)(2,1)S(1)} async-done(((bf16[8,384,384]{2,1,0:T(8,128)(2,1)}), bf16[8,384,384]{2,1,0:T(8,128)(2,1)S(1)}, u32[]{:S(2)}, u32[]{:S(2)}) %all-to-all-start.1) | async-done | bytes 2359328 | tf_op jit(solution)/shard_map/all_to_all | solution.py:258
  75.6 1.6 %fusion = f32[2,384,384]{2,0,1:T(2,128)S(1)} fusion(bf16[8,384,384]{2,1,0:T(8,128)(2,1)S(1)} %all-to-all-done.1, s32[8]{0:T(128)S(1)} %reduce), kind=kOutput, calls=%fused_computation | convolution fusion | flops 4718608 | bytes 3538976 | tf_op jit(solution)/shard_map/sc,sxy->cxy/dot_general | solution.py:27
  77.2 0.9 %fusion.29 = (f32[1,384,384]{2,0,1:T(1,128)S(1)}, f32[1,384,384]{2,0,1:T(1,128)S(1)}) fusion(f32[2,384,384]{2,0,1:T(2,128)S(1)} %fusion), kind=kLoop, calls=%fused_computation.73 | loop fusion | bytes 2359296 | tf_op jit(solution)/shard_map/slice | solution.py:266
  78.3 1.3 %collective-permute-start = (bf16[64,704]{1,0:T(8,128)(2,1)S(1)}, bf16[64,704]{1,0:T(8,128)(2,1)S(1)}, u32[]{:S(2)}, u32[]{:S(2)}) collective-permute-start(bf16[64,704]{1,0:T(8,128)(2,1)S(1)} %fusion.11), channel_id=1, source_target_pairs={{1,0},{2,1},{3,2},{4,3},{5,4},{6,5},{7,6},{9,8},{10,9},{11,10},{12... | collective-permute-start | bytes 270344 | tf_op jit(solution)/shard_map/ppermute | solution.py:23
  79.6 0.2 fusion.4
  79.8 1.7 %collective-permute-done = bf16[64,704]{1,0:T(8,128)(2,1)S(1)} collective-permute-done((bf16[64,704]{1,0:T(8,128)(2,1)S(1)}, bf16[64,704]{1,0:T(8,128)(2,1)S(1)}, u32[]{:S(2)}, u32[]{:S(2)}) %collective-permute-start) | collective-permute-done | bytes 90144 | tf_op jit(solution)/shard_map/ppermute | solution.py:23
  81.6 1.3 %collective-permute-start.1 = (bf16[320,64]{1,0:T(8,128)(2,1)S(1)}, bf16[320,64]{1,0:T(8,128)(2,1)S(1)}, u32[]{:S(2)}, u32[]{:S(2)}) collective-permute-start(bf16[320,64]{1,0:T(8,128)(2,1)S(1)} %fusion.14), channel_id=1, source_target_pairs={{8,0},{16,8},{24,16},{9,1},{17,9},{25,17},{10,2},{18,10},{26,18},{... | collective-permute-start | bytes 122888 | tf_op jit(solution)/shard_map/ppermute | solution.py:23
  82.9 0.3 fusion.3
  83.2 5.0 %collective-permute-done.1 = bf16[320,64]{1,0:T(8,128)(2,1)S(1)} collective-permute-done((bf16[320,64]{1,0:T(8,128)(2,1)S(1)}, bf16[320,64]{1,0:T(8,128)(2,1)S(1)}, u32[]{:S(2)}, u32[]{:S(2)}) %collective-permute-start.1) | collective-permute-done | bytes 40992 | tf_op jit(solution)/shard_map/ppermute | solution.py:23
  88.2 1.0 %pad_maximum_fusion.2 = f32[320,640]{1,0:T(8,128)} fusion(f32[320,64]{1,0:T(8,128)S(1)} %fusion.13, f32[320,576]{1,0:T(8,128)S(1)} %fusion.3), kind=kLoop, calls=%fused_computation.15 | loop fusion | flops 204800 | bytes 1638400 | tf_op jit(solution)/shard_map/concatenate | solution.py:232
  (33 shorter events, 0.9 us)
Async XLA Ops:
  0.0 8.6 %copy-start.1 = (f32[384,384]{1,0:T(8,128)S(1)}, f32[384,384]{1,0:T(8,128)}, u32[]{:S(2)}) copy-start(f32[384,384]{1,0:T(8,128)} %param.13) | copy-start | bytes 1769476
  2.2 39.8 %all-to-all-start = ((s32[8,1,1]{2,1,0:T(1,128)}), s32[8,1,1]{2,1,0:T(1,128)S(1)}, u32[]{:S(2)}, u32[]{:S(2)}) async-start(s32[8,1,1]{2,1,0:T(1,128)} %copy.15), calls=%async_computation | async-start | bytes 8192 | tf_op jit(solution)/shard_map/all_to_all | solution.py:259
  7.4 1.3 %copy-start.3 = (s32[1,3]{1,0:T(1,128)S(1)}, s32[1,3]{1,0:T(1,128)}, u32[]{:S(2)}) copy-start(s32[1,3]{1,0:T(1,128)} %param.11) | copy-start | bytes 40
  7.4 2.0 %slice-start = ((f32[384,384]{1,0:T(8,128)}), f32[1,384]{1,0:T(1,128)S(1)}, s32[]{:S(2)}) async-start(f32[384,384]{1,0:T(8,128)} %param.12), calls=%async_computation.2 | async-start | bytes 3072 | tf_op jit(solution)/shard_map/jit(_roll_static)/slice | solution.py:171
  7.4 2.3 %slice-start.1 = ((f32[384,384]{1,0:T(8,128)}), f32[1,384]{1,0:T(1,128)S(1)}, s32[]{:S(2)}) async-start(f32[384,384]{1,0:T(8,128)} %param.13), calls=%async_computation.3 | async-start | bytes 3072 | tf_op jit(solution)/shard_map/jit(_roll_static)/slice | solution.py:171
  7.4 2.5 %copy-start.4 = (f32[1,3,1]{1,2,0:T(1,128)S(1)}, f32[1,3,1]{1,2,0:T(1,128)}, u32[]{:S(2)}) copy-start(f32[1,3,1]{1,2,0:T(1,128)} %param.10) | copy-start | bytes 40
  7.4 3.5 %copy-start.2 = (s32[1,3,12,12]{3,0,2,1:T(1,128)S(1)}, s32[1,3,12,12]{3,0,2,1:T(1,128)}, u32[]{:S(2)}) copy-start(s32[1,3,12,12]{3,0,2,1:T(1,128)} %param.9) | copy-start | bytes 5188
  14.9 1.1 %copy-start = (f32[384,384]{1,0:T(8,128)S(1)}, f32[384,384]{1,0:T(8,128)}, u32[]{:S(2)}) copy-start(f32[384,384]{1,0:T(8,128)} %param.12) | copy-start | bytes 1769476
  42.0 33.6 %all-to-all-start.1 = ((bf16[8,384,384]{2,1,0:T(8,128)(2,1)}), bf16[8,384,384]{2,1,0:T(8,128)(2,1)S(1)}, u32[]{:S(2)}, u32[]{:S(2)}) async-start(bf16[8,384,384]{2,1,0:T(8,128)(2,1)} %copy.18), calls=%async_computation.1 | async-start | bytes 4718592 | tf_op jit(solution)/shard_map/all_to_all | solution.py:258
  78.3 3.2 %collective-permute-start = (bf16[64,704]{1,0:T(8,128)(2,1)S(1)}, bf16[64,704]{1,0:T(8,128)(2,1)S(1)}, u32[]{:S(2)}, u32[]{:S(2)}) collective-permute-start(bf16[64,704]{1,0:T(8,128)(2,1)S(1)} %fusion.11), channel_id=1, source_target_pairs={{1,0},{2,1},{3,2},{4,3},{5,4},{6,5},{7,6},{9,8},{10,9},{11,10},{12... | collective-permute-start | bytes 270344 | tf_op jit(solution)/shard_map/ppermute | solution.py:23
  81.6 6.5 %collective-permute-start.1 = (bf16[320,64]{1,0:T(8,128)(2,1)S(1)}, bf16[320,64]{1,0:T(8,128)(2,1)S(1)}, u32[]{:S(2)}, u32[]{:S(2)}) collective-permute-start(bf16[320,64]{1,0:T(8,128)(2,1)S(1)} %fusion.14), channel_id=1, source_target_pairs={{8,0},{16,8},{24,16},{9,1},{17,9},{25,17},{10,2},{18,10},{26,18},{... | collective-permute-start | bytes 122888 | tf_op jit(solution)/shard_map/ppermute | solution.py:23

commit v2 on v1

--- a/solution.py
+++ b/solution.py
@@ -15,16 +15,6 @@
 wiener = 0.1
 pattern_base = (37, 101)
 pattern_step = (29, -53)
-
-
-def passed_along(value, axis, steps):
-    count = lax.axis_size(axis)
-    leading, last = (max(0, -steps), min(count, count - steps))
-    return lax.ppermute(value, axis, [(source, source + steps) for source in range(leading, last)])
-
-
-def batched(pattern, operand_a, operand_b):
-    return jnp.einsum(pattern, operand_a, operand_b, preferred_element_type=jnp.float32)
 
 
 def pattern_shift(orient):
@@ -51,16 +41,77 @@
 
 
 def tile_kernel(
-    phase_count, cells, intersection,
-    coef_ref, flags_ref, frames_ref, mask_ref, right_ref, left_ref, otf_ref, apod_ref,
+    phase_count, cells, intersection, slot_count, bits,
+    coef_ref, flags_ref, frames_ref, mask_ref, right_ref, left_ref, otf_ref, apod_ref, label_ref,
     out_ref,
-    wide_ref, gain_ref, images_ref, waves_ref, spec_ref, mid_ref,
+    wide_ref, gain_ref, images_ref, waves_ref, spec_ref, mid_ref, tile_ref, twin_ref, cand_ref,
+    names_ref, keep_ref, pack_ref, land_ref, hand_ref, final_ref, full_ref, up_ref, from_down_ref,
+    from_right_ref, from_corner_ref, name_sems, twin_sems, cand_sems, pack_sems, final_sems, fold_sems,
 ):
+    me = lax.axis_index("ty")
+    count = lax.axis_size("ty")
+    group = lax.axis_index("tx")
+    groups = lax.axis_size("tx")
+    half = lax.rem(me, 2)
+    routes = (tuple(range(1, bits)), tuple(reversed(range(1, bits))))
+
+    def across(mask):
+        other = me
+        for bit in range(bits):
+            if mask >> bit & 1:
+                other = other + (1 << bit) - 2 * (1 << bit) * lax.rem(me // (1 << bit), 2)
+        return (group, other)
+
+    up = lax.rem(me + count - 1, count)
+    down = lax.rem(me + 1, count)
+    before = lax.rem(group + groups - 1, groups)
+    after = lax.rem(group + 1, groups)
+    name_masks = [1] + [(1 << route[0]) | low for route in routes for low in (0, 1)]
+    greeted = [across(mask) for mask in name_masks]
+    greeted += [across(1 << bit) for bit in range(2, bits - 1)]
+    greeted += [(group, up), (group, down), (before, me), (after, me), (before, up), (after, down)]
+
+    def sent(src, dst, sems, index, target):
+        return pltpu.make_async_remote_copy(
+            src_ref=src, dst_ref=dst, send_sem=sems.at[(0,) + index], recv_sem=sems.at[(1,) + index],
+            device_id=target, device_id_type=pl.DeviceIdType.MESH,
+        )
+
     step = pl.program_id(0)
     length = otf_ref.shape[-1]
     halfway = phase_count // 2
     shift_rows, shift_cols = pattern_shift(0)
     chunk = length // 3
+    part = length // 4
+    own_rows = pl.multiple_of(half * (2 * part), 2 * part)
+    twin_rows = pl.multiple_of((1 - half) * (2 * part), 2 * part)
+
+    def name_copy(place):
+        return sent(label_ref, names_ref.at[place], name_sems, (place,), across(name_masks[place]))
+
+    def twin_copy(slot):
+        return sent(tile_ref.at[slot, pl.ds(twin_rows, 2 * part)], twin_ref.at[slot], twin_sems, (slot,), across(1))
+
+    def first_copy(slot, piece, who):
+        if who == 0:
+            src = tile_ref.at[slot, pl.ds(pl.multiple_of(own_rows + piece * part, part), part)]
+        else:
+            src = twin_ref.at[slot, pl.ds(piece * part, part)]
+        return sent(src, cand_ref.at[piece, slot, who], cand_sems, (piece, slot, who), across(1 << routes[piece][0]))
+
+    def relay(slot):
+        twin_copy(slot).wait_recv()
+        for piece in range(2):
+            first_copy(slot, piece, 1).start()
+
+    @pl.when(step == 0)
+    def _():
+        barrier = pltpu.get_barrier_semaphore()
+        for target in greeted:
+            pl.semaphore_signal(barrier, inc=1, device_id=target, device_id_type=pl.DeviceIdType.MESH)
+        pl.semaphore_wait(barrier, len(greeted))
+        for place in range(len(name_masks)):
+            name_copy(place).start()
 
     @pl.when(step == 0)
     def _():
@@ -112,12 +163,16 @@
             total = total + planes[p]
         images_ref[0, rows, :length] = (total * (1.0 / phase_count)).astype(jnp.bfloat16)
         for m in range(1, halfway + 1):
-            for part in range(2):
-                base = ((step * (halfway + 1) + m) * 2 + part) * phase_count
+            for side in range(2):
+                base = ((step * (halfway + 1) + m) * 2 + side) * phase_count
                 total = planes[0] * coef_ref[base]
                 for p in range(1, phase_count):
                     total = total + planes[p] * coef_ref[base + p]
-                images_ref[m, rows, part * length:(part + 1) * length] = total.astype(jnp.bfloat16)
+                images_ref[m, rows, side * length:(side + 1) * length] = total.astype(jnp.bfloat16)
+
+    @pl.when(step > 0)
+    def _():
+        relay(step - 1)
 
     for m in range(halfway + 1):
         for third in range(3):
@@ -164,14 +219,160 @@
         places = lax.broadcasted_iota(jnp.int32, (chunk, length), 0) + third * chunk
         picture = picture * ramp(places, row_last)
         picture = picture * ramp(lax.broadcasted_iota(jnp.int32, (chunk, length), 1), column_last)
-        out_ref[0, rows, :] = jnp.where(held, picture, 0.0).astype(jnp.bfloat16)
+        tile_ref[step, rows, :] = jnp.where(held, picture, 0.0).astype(jnp.bfloat16)
+
+    twin_copy(step).start()
+    for piece in range(2):
+        first_copy(step, piece, 0).start()
+
+    @pl.when(step == slot_count - 1)
+    def _():
+        relay(slot_count - 1)
+        for place in range(len(name_masks)):
+            name_copy(place).wait()
+
+        def candidate(piece, who, slot):
+            if who == 0:
+                return tile_ref[slot, pl.ds(pl.multiple_of(own_rows + piece * part, part), part), :]
+            if who == 1:
+                return twin_ref[slot, pl.ds(piece * part, part), :]
+            return cand_ref[piece, slot, who - 2]
+
+        def labels(piece, who, slot):
+            if who == 0:
+                return label_ref[slot:slot + 1, :]
+            place = 0 if who == 1 else 1 + 2 * piece + (who - 2)
+            return names_ref[place, slot:slot + 1, :]
+
+        def combos(free):
+            masks = [0]
+            for bit in free:
+                masks = masks + [mask | (1 << bit) for mask in masks]
+            return masks
+
+        def packed(piece, mask, column):
+            wanted = across(mask)[1] * GROUP_COLS + column
+            total = None
+            for slot in range(slot_count):
+                for who in range(4):
+                    hit = jnp.where(labels(piece, who, slot) == wanted, 1.0, 0.0).astype(jnp.bfloat16)
+                    term = candidate(piece, who, slot) * hit
+                    total = term if total is None else total + term
+            return total
+
+        def pack_copy(piece, hop):
+            size = GROUP_COLS << (len(routes[piece]) - hop)
+            return sent(
+                pack_ref.at[piece, hop - 1, pl.ds(0, size)], land_ref.at[piece, hop - 1, pl.ds(0, size)],
+                pack_sems, (piece, hop - 1), across(1 << routes[piece][hop]),
+            )
+
+        for piece in range(2):
+            for slot in range(slot_count):
+                for who in range(2):
+                    first_copy(slot, piece, who).wait_recv()
+            route = routes[piece]
+            rest = combos((0,) + route[2:])
+            for place, mask in enumerate(rest):
+                for column in range(GROUP_COLS):
+                    pack_ref[piece, 0, place * GROUP_COLS + column] = packed(piece, mask | (1 << route[1]), column)
+            pack_copy(piece, 1).start()
+        for piece in range(2):
+            for place, mask in enumerate(combos((0,) + routes[piece][2:])):
+                for column in range(GROUP_COLS):
+                    keep_ref[piece, place * GROUP_COLS + column] = packed(piece, mask, column)
+        for hop in range(1, bits - 1):
+            for piece in range(2):
+                pack_copy(piece, hop).wait_recv()
+                size = GROUP_COLS << (bits - 1 - hop)
+                if hop < bits - 2:
+                    held_order = combos((0,) + routes[piece][hop + 1:])
+                    later = combos((0,) + routes[piece][hop + 2:])
+                    bit = 1 << routes[piece][hop + 1]
+                    for place, mask in enumerate(later):
+                        there = held_order.index(mask | bit)
+                        here = held_order.index(mask)
+                        for column in range(GROUP_COLS):
+                            i, j, k = (there * GROUP_COLS + column, here * GROUP_COLS + column, place * GROUP_COLS + column)
+                            pack_ref[piece, hop, k] = keep_ref[piece, i] + land_ref[piece, hop - 1, i]
+                            keep_ref[piece, k] = keep_ref[piece, j] + land_ref[piece, hop - 1, j]
+                    pack_copy(piece, hop + 1).start()
+                else:
+                    for column in range(GROUP_COLS):
+                        hand_ref[piece, column] = keep_ref[piece, GROUP_COLS + column] + land_ref[piece, hop - 1, GROUP_COLS + column]
+                    sent(hand_ref.at[piece], final_ref.at[piece], final_sems, (piece,), across(1)).start()
+        for piece in range(2):
+            rows = pl.ds(pl.multiple_of(own_rows + piece * part, part), part)
+            for column in range(GROUP_COLS):
+                full_ref[column, rows, :] = keep_ref[piece, column] + land_ref[piece, bits - 3, column]
+        for piece in range(2):
+            sent(hand_ref.at[piece], final_ref.at[piece], final_sems, (piece,), across(1)).wait_recv()
+            rows = pl.ds(pl.multiple_of(twin_rows + piece * part, part), part)
+            for column in range(GROUP_COLS):
+                full_ref[column, rows, :] = final_ref[piece, column]
+
+        side = 2 * intersection
+        inner = length - intersection
+        top = pl.ds(0, intersection)
+        low = pl.ds(intersection, inner)
+
+        fold_left = sent(full_ref.at[0, low, pl.ds(0, side)], from_right_ref, fold_sems, (0,), (before, me))
+        fold_corner = sent(full_ref.at[0, top, pl.ds(0, side)], from_corner_ref, fold_sems, (1,), (before, up))
+        fold_up = sent(up_ref, from_down_ref, fold_sems, (2,), (group, up))
+        fold_left.start()
+        fold_corner.start()
+
+        def panel(rows, size):
+            total = None
+            for column in range(GROUP_COLS):
+                value = full_ref[column, rows, :].astype(jnp.float32)
+                start = STRIDE * column - intersection
+                if start < 0:
+                    value = value[:, -start:]
+                    start = 0
+                ends = [jnp.zeros((size, start), jnp.float32), value]
+                ends.append(jnp.zeros((size, STRIDE * GROUP_COLS - start - value.shape[1]), jnp.float32))
+                value = jnp.concatenate([piece for piece in ends if piece.shape[1]], axis=1)
+                total = value if total is None else total + value
+            return total
+
+        up_ref[...] = panel(top, intersection).astype(jnp.bfloat16)
+        fold_up.start()
+        out_ref[...] = panel(low, inner)
+        wide = STRIDE * GROUP_COLS
+        not_low = jnp.where(me < count - 1, 1.0, 0.0)
+        not_right = jnp.where(group < groups - 1, 1.0, 0.0)
+        tail_rows = pl.ds(inner - intersection, intersection)
+
+        def at_right(value):
+            return jnp.concatenate([jnp.zeros((value.shape[0], side - intersection), jnp.float32), value[:, :intersection].astype(jnp.float32)], axis=1)
+
+        fold_left.wait_recv()
+        out_ref[:, wide - side:] = out_ref[:, wide - side:] + at_right(from_right_ref[...]) * not_right
+        fold_up.wait_recv()
+        out_ref[tail_rows, :] = out_ref[tail_rows, :] + from_down_ref[...].astype(jnp.float32) * not_low
+        fold_corner.wait_recv()
+        out_ref[tail_rows, wide - side:] = out_ref[tail_rows, wide - side:] + at_right(from_corner_ref[...]) * (not_right * not_low)
+
+        for slot in range(slot_count):
+            twin_copy(slot).wait_send()
+            for piece in range(2):
+                for who in range(2):
+                    first_copy(slot, piece, who).wait_send()
+        for piece in range(2):
+            for hop in range(1, bits - 1):
+                pack_copy(piece, hop).wait_send()
+            sent(hand_ref.at[piece], final_ref.at[piece], final_sems, (piece,), across(1)).wait_send()
+        fold_left.wait_send()
+        fold_corner.wait_send()
+        fold_up.wait_send()
 
 
 def reversed_map(value):
     return jnp.roll(value[::-1, ::-1], (1, 1), (0, 1))
 
 
-def tile_results(frames, masks, phases, own_tiles, otf, apod, row_last, column_last, intersection):
+def stitched_block(frames, masks, phases, own_tiles, otf, apod, row_last, column_last, intersection):
     slot_count, phase_count = (frames.shape[1], frames.shape[3])
     length = otf.shape[0]
     cells = masks.shape[-1]
@@ -186,22 +387,30 @@
     otfs = jnp.stack([otf, reversed_map(otf)])
     apods = jnp.stack([apod, reversed_map(apod)])
     bands = halfway + 1
+    count = lax.axis_size("ty")
+    bits = count.bit_length() - 1
+    part = length // 4
+    wide = STRIDE * GROUP_COLS
+    slot_rows = -(-slot_count // 8) * 8
+    names = jnp.broadcast_to(jnp.pad(own_tiles, (0, slot_rows - slot_count), constant_values=-1)[:, None], (slot_rows, length))
+    most = GROUP_COLS << (bits - 2)
+    dma = pltpu.SemaphoreType.DMA
 
     def whole(array):
         return pl.BlockSpec(array.shape, lambda s: (0,) * array.ndim)
 
     return pl.pallas_call(
-        lambda *refs: tile_kernel(phase_count, cells, intersection, *refs),
+        lambda *refs: tile_kernel(phase_count, cells, intersection, slot_count, bits, *refs),
         grid=(slot_count,),
         in_specs=[
             pl.BlockSpec(memory_space=pltpu.SMEM),
             pl.BlockSpec(memory_space=pltpu.SMEM),
             pl.BlockSpec((1, 1) + frames.shape[2:], lambda s: (0, s, 0, 0, 0, 0)),
             pl.BlockSpec((1, cells, length), lambda s: (s, 0, 0)),
-            whole(right), whole(left), whole(otfs), whole(apods),
+            whole(right), whole(left), whole(otfs), whole(apods), whole(names),
         ],
-        out_specs=pl.BlockSpec((1, length, length), lambda s: (s, 0, 0)),
-        out_shape=jax.ShapeDtypeStruct((slot_count, length, length), jnp.bfloat16),
+        out_specs=pl.BlockSpec((STRIDE, wide), lambda s: (0, 0)),
+        out_shape=jax.ShapeDtypeStruct((STRIDE, wide), jnp.float32),
         scratch_shapes=[
             pltpu.VMEM((bands, 2 * length, 2 * length), jnp.bfloat16),
             pltpu.VMEM((2 * halfway + 1, length, length), jnp.float32),
@@ -209,27 +418,31 @@
             pltpu.VMEM((bands, 2 * length, 2 * length), jnp.bfloat16),
             pltpu.VMEM((length, 2 * length), jnp.bfloat16),
             pltpu.VMEM((2 * length, length), jnp.bfloat16),
+            pltpu.VMEM((slot_count, length, length), jnp.bfloat16),
+            pltpu.VMEM((slot_count, 2 * part, length), jnp.bfloat16),
+            pltpu.VMEM((2, slot_count, 2, part, length), jnp.bfloat16),
+            pltpu.VMEM((5, slot_rows, length), jnp.int32),
+            pltpu.VMEM((2, most, part, length), jnp.bfloat16),
+            pltpu.VMEM((2, bits - 2, most, part, length), jnp.bfloat16),
+            pltpu.VMEM((2, bits - 2, most, part, length), jnp.bfloat16),
+            pltpu.VMEM((2, GROUP_COLS, part, length), jnp.bfloat16),
+            pltpu.VMEM((2, GROUP_COLS, part, length), jnp.bfloat16),
+            pltpu.VMEM((GROUP_COLS, length, length), jnp.bfloat16),
+            pltpu.VMEM((intersection, wide), jnp.bfloat16),
+            pltpu.VMEM((intersection, wide), jnp.bfloat16),
+            pltpu.VMEM((length - intersection, 2 * intersection), jnp.bfloat16),
+            pltpu.VMEM((intersection, 2 * intersection), jnp.bfloat16),
+            dma((2, 5)),
+            dma((2, slot_count)),
+            dma((2, 2, slot_count, 2)),
+            dma((2, 2, bits - 2)),
+            dma((2, 2)),
+            dma((2, 3)),
         ],
-        compiler_params=pltpu.CompilerParams(vmem_limit_bytes=60 * 1024 * 1024),
-    )(coef.reshape(-1), flags.reshape(-1), frames, mask_rows, right, left, otfs, apods)
-
-
-def fold_rows(padded_block, intersection):
-    arrived = passed_along(padded_block[:intersection].astype(jnp.bfloat16), "ty", -1).astype(
-        jnp.float32
-    )
-    interior = padded_block[intersection:]
-    keep_rows = interior.shape[0] - intersection
-    return jnp.concatenate([interior[:keep_rows], interior[keep_rows:] + arrived], axis=0)
-
-
-def fold_columns(padded_block, intersection):
-    arrived = passed_along(padded_block[:, :intersection].astype(jnp.bfloat16), "tx", -1).astype(
-        jnp.float32
-    )
-    interior = padded_block[:, intersection:]
-    keep_cols = interior.shape[1] - intersection
-    return jnp.concatenate([interior[:, :keep_cols], interior[:, keep_cols:] + arrived], axis=1)
+        compiler_params=pltpu.CompilerParams(
+            vmem_limit_bytes=60 * 1024 * 1024, collective_id=0, has_side_effects=True
+        ),
+    )(coef.reshape(-1), flags.reshape(-1), frames, mask_rows, right, left, otfs, apods, names)
 
 
 def shards(frames, masks, phases, slot_tile, otf, apod):
@@ -242,32 +455,10 @@
 
     tile_rows = own_tiles // GROUP_COLS
     columns = GROUP_COLS * my_group + own_tiles % GROUP_COLS
-    results = tile_results(
+    return stitched_block(
         frames, masks, phases, own_tiles, otf, apod,
         tile_rows == row_count - 1, columns == GROUP_COLS * group_count - 1, intersection,
     )
-    column_places = jnp.arange(GROUP_COLS, dtype=jnp.int32)
-    owner_rows = jnp.arange(row_count, dtype=jnp.int32)
-    matches = ((own_tiles // GROUP_COLS)[:, None] == owner_rows[None, :]) & (own_tiles >= 0)[
-        :, None
-    ]
-    choose = matches.astype(jnp.bfloat16)
-    outgoing = batched("sh,sxy->hxy", choose, results).astype(jnp.bfloat16)
-    labels = jnp.sum(matches.astype(jnp.int32) * (own_tiles % GROUP_COLS + 1)[:, None], axis=0) - 1
-    incoming, column_tags = (
-        lax.all_to_all(outgoing, "ty", split_axis=0, concat_axis=0, tiled=True),
-        lax.all_to_all(labels[:, None], "ty", split_axis=0, concat_axis=0, tiled=True),
-    )
-    selector = (column_tags == column_places[None, :]).astype(jnp.bfloat16)
-    tiles_here = batched("sc,sxy->cxy", selector, incoming)
-    padded = jnp.zeros((length, STRIDE * GROUP_COLS + intersection), jnp.float32)
-    for column_place in range(GROUP_COLS):
-        padded = padded + jnp.pad(
-            tiles_here[column_place],
-            ((0, 0), (STRIDE * column_place, STRIDE * (GROUP_COLS - 1 - column_place))),
-        )
-    stitched = fold_columns(fold_rows(padded, intersection), intersection)
-    return stitched
 
 
 def solution(mesh):

time: 89.6 us -> 58.6 us (0.65)
  waiting for transfers between devices: 35.8 us -> 0 us
  Pallas kernels: 18.3 us -> 44.5 us
  starting transfers between devices: 12 us -> 0 us
  matrix products: 5.97 us -> 0 us
  other arithmetic: 5.9 us -> 3.81 us
  local copies, waits for them, and re-layouts: 11 us -> 9.97 us
    all_to_all x2 -> x0, waiting for transfers between devices: 29.2 us -> none  [the longest x1 29.2 us: shards(): lax.all_to_all(outgoing, 'ty', split_axis=0, concat_axis=0, tiled=True)]
    pallas_call x1, Pallas kernels: 18.3 us -> 44.5 us  [stitched_block(): pl.pallas_call(lambda *refs: tile_kernel(phase_count, cells, intersection...]
    all_to_all x2 -> x0, starting transfers between devices: 9.39 us -> none  [the longest x1 5.2 us: shards(): lax.all_to_all(labels[:, None], 'ty', split_axis=0, concat_axis=0, tiled=...]
    ppermute x2 -> x0, waiting for transfers between devices: 6.65 us -> none  [passed_along(): lax.ppermute(value, axis, [(source, source + steps) for source in range(l...]
    dot_general x2 -> x0, matrix products: 5.97 us -> none  [batched(): jnp.einsum(pattern, operand_a, operand_b, preferred_element_type=jnp.floa...]
    ppermute x2 -> x0, starting transfers between devices: 2.58 us -> none  [passed_along(): lax.ppermute(value, axis, [(source, source + steps) for source in range(l...]
    convert_element_type x3 -> x2, local copies, waits for them, and re-layouts: 2.44 us -> 0.74 us  [stitched_block(): jnp.stack([own_tiles >= 0, row_last, column_last], axis=1).astype(jnp.int32)]
    unnamed x13 -> x10, local copies, waits for them, and re-layouts: 0.62 us -> 2.12 us
  transfers between devices with their start and end apart: 4 -> 0, of which waited for: 3 -> 0; matrix products, arithmetic and copies ran while one was open for 18% -> 0% of each run, Pallas kernels for 20% -> 0%
where the time goes in v2:
time: 58.6 us; the launch traced here: 58.4 us
  Pallas kernels  44.5 us (76%)
  local copies, waits for them, and re-layouts  9.97 us (17%)
  other arithmetic  3.81 us (7%)
    pallas_call x1, Pallas kernels, stitched_block(): pl.pallas_call(lambda *refs: tile_kernel(phase_count, cells, intersection...  44.5 us
    slice x10, local copies, waits for them, and re-layouts, reversed_map(): return jnp.roll(value[::-1, ::-1], (1, 1), (0, 1))  4.91 us
    unnamed x10, local copies, waits for them, and re-layouts  2.12 us
    another operation x2, other arithmetic, stitched_block(): otfs = jnp.stack([otf, reversed_map(otf)])  1.88 us

profile of v2, /device:TPU:0, one launch (start us, length us, event | category | flops | bytes accessed | tf_op | source)
XLA Modules:
  0.0 58.4 jit_solution(1316482987176509475)
XLA Ops:
  0.0 0.7 %bitcast_compare_fusion = (pred[3,1]{0,1:T(4,128)(4,1)S(1)}, pred[3,1]{0,1:T(4,128)(4,1)S(1)}, pred[3,1]{0,1:T(4,128)(4,1)S(1)}) fusion(s32[1,3]{1,0:T(1,128)} %param.11, s32[]{:T(128)S(6)} %mul.38), kind=kLoop, calls=%fused_computation.25 | loop fusion | flops 69 | bytes 25 | tf_op jit(solution)/shard_map/ge | solution.py:384
  0.7 0.1 copy.9
  0.8 0.7 %reshape.182.refs_1_ = s32[9]{0:T(128)} reshape(s32[3,3]{1,0:T(4,128)S(1)} %copy.9) | data formatting | bytes 72 | tf_op jit(solution)/shard_map/convert_element_type | solution.py:384
  1.4 0.7 %broadcast_add_fusion = f32[3,5]{1,0:T(4,128)S(1)} fusion(f32[5]{0:T(128)S(1)} %convert_multiply_fusion, f32[3]{0:T(128)} %bitcast.33), kind=kLoop, calls=%fused_computation.21 | loop fusion | flops 15 | bytes 92 | tf_op jit(solution)/shard_map/add | solution.py:382
  2.2 0.2 multiply_cosine_fusion
  2.4 0.6 %div.20.refs_0_ = f32[90]{0:T(128)} reshape(f32[3,3,2,5]{3,2,1,0:T(2,128)S(1)} %maximum_multiply_fusion) | data formatting | bytes 720 | tf_op jit(solution)/shard_map/div | solution.py:383
  3.0 0.0 slice-start.1
  3.0 1.2 %slice.48 = f32[383,384]{1,0:T(8,128)S(1)} slice(f32[384,384]{1,0:T(8,128)} %param.13), slice={[1:384], [0:384]} | slice | bytes 1176576 | tf_op jit(solution)/shard_map/jit(_roll_static)/slice | solution.py:372
  4.2 0.0 copy-start
  4.2 1.5 %slice.49 = f32[383,384]{1,0:T(8,128)S(1)} reverse(f32[383,384]{1,0:T(8,128)S(1)} %slice.48), dimensions={0,1} | reverse | bytes 1176576 | tf_op jit(solution)/shard_map/jit(_roll_static)/slice | solution.py:372
  5.8 0.0 slice-done.1
  5.8 0.3 slice.47
  6.1 0.3 fusion.1
  6.4 0.0 copy-done
  6.4 0.0 slice-start
  6.4 0.0 copy-start.1
  6.4 1.5 %slice.43 = f32[383,384]{1,0:T(8,128)S(1)} reverse(f32[383,384]{1,0:T(8,128)S(1)} %slice.42), dimensions={0,1} | reverse | bytes 1176576 | tf_op jit(solution)/shard_map/jit(_roll_static)/slice | solution.py:372
  8.0 0.0 slice-done
  8.0 0.3 slice.41
  8.3 0.3 fusion.3
  8.6 0.0 copy-done.1
  8.6 0.0 copy-start.2
  8.6 0.0 copy-start.3
  8.6 1.6 %pad_maximum_fusion = (f32[2,384,384]{2,1,0:T(8,128)}, f32[2,384,384]{2,1,0:T(8,128)}) fusion(f32[1,384,384]{2,1,0:T(8,128)S(1)} %fusion.3, f32[1,384,384]{2,1,0:T(8,128)S(1)} %bitcast.29, f32[1,384,384]{2,1,0:T(8,128)S(1)} %fusion.1, f32[1,384,384]{2,1,0:T(8,128)S(1)} %bitcast.30), kind=kLoop, calls=%fused_computation | loop fusion | flops 589824 | bytes 4718592 | tf_op jit(solution)/shard_map/stack | solution.py:387
  10.2 0.0 copy-done.2
  10.2 0.1 broadcast_in_dim.4
  10.4 0.8 %reshape.181.refs_3_ = bf16[3,12,384]{2,1,0:T(8,128)(2,1)} reshape(bf16[3,12,12,32]{3,2,1,0:T(8,128)(2,1)S(1)} %broadcast_in_dim.4) | data formatting | bytes 55296 | tf_op jit(solution)/shard_map/reshape | solution.py:385
  11.2 0.0 copy-done.3
  11.2 0.7 %broadcast_in_dim.5.refs_8_ = s32[8,384]{1,0:T(8,128)} broadcast(s32[8]{0:T(128)S(1)} %pad.4), dimensions={0} | broadcast | bytes 12320 | tf_op jit(solution)/shard_map/broadcast_in_dim | solution.py:395
  11.8 44.5 %shard_map.82 = f32[320,640]{1,0:T(8,128)} custom-call(f32[90]{0:T(128)} %div.20.refs_0_, s32[9]{0:T(128)} %reshape.182.refs_1_, bf16[1,3,1,5,384,384]{5,4,3,2,1,0:T(8,128)(2,1)} %refs_2_.1, bf16[3,12,384]{2,1,0:T(8,128)(2,1)} %reshape.181.refs_3_, bf16[3,384,768]{2,1,0:T(8,128)(2,1)} %constant.44.clone.refs_4_, ...), custom_call_target="tpu_custom_call" | custom-call | tf_op jit(solution)/shard_map/pallas_call | solution.py:402
  56.3 2.1 %copy.14 = f32[320,640]{1,0:T(8,128)} copy(f32[320,640]{1,0:T(8,128)} %shard_map.82) | data formatting | bytes 1638400
  (8 shorter events, 0.1 us)
Async XLA Ops:
  3.0 2.7 %slice-start.1 = ((f32[384,384]{1,0:T(8,128)}), f32[1,384]{1,0:T(1,128)S(1)}, s32[]{:S(2)}) async-start(f32[384,384]{1,0:T(8,128)} %param.13), calls=%async_computation.1 | async-start | bytes 3072 | tf_op jit(solution)/shard_map/jit(_roll_static)/slice | solution.py:372
  4.2 2.1 %copy-start = (f32[384,384]{1,0:T(8,128)S(1)}, f32[384,384]{1,0:T(8,128)}, u32[]{:S(2)}) copy-start(f32[384,384]{1,0:T(8,128)} %param.12) | copy-start | bytes 1769476
  6.4 1.6 %slice-start = ((f32[384,384]{1,0:T(8,128)}), f32[1,384]{1,0:T(1,128)S(1)}, s32[]{:S(2)}) async-start(f32[384,384]{1,0:T(8,128)} %param.12), calls=%async_computation | async-start | bytes 3072 | tf_op jit(solution)/shard_map/jit(_roll_static)/slice | solution.py:372
  6.4 2.1 %copy-start.1 = (f32[384,384]{1,0:T(8,128)S(1)}, f32[384,384]{1,0:T(8,128)}, u32[]{:S(2)}) copy-start(f32[384,384]{1,0:T(8,128)} %param.13) | copy-start | bytes 1769476
  8.6 1.6 %copy-start.2 = (s32[1,3,12,12]{3,0,2,1:T(1,128)S(1)}, s32[1,3,12,12]{3,0,2,1:T(1,128)}, u32[]{:S(2)}) copy-start(s32[1,3,12,12]{3,0,2,1:T(1,128)} %param.9) | copy-start | bytes 5188
  8.6 2.6 %copy-start.3 = (s32[1,3]{1,0:T(1,128)S(1)}, s32[1,3]{1,0:T(1,128)}, u32[]{:S(2)}) copy-start(s32[1,3]{1,0:T(1,128)} %param.11) | copy-start | bytes 40

commit v3 on v2

--- a/solution.py
+++ b/solution.py
@@ -32,7 +32,7 @@
         left.append(np.concatenate([np.roll(cosine, -m * rows, 0), np.roll(sine, -m * rows, 0)], 1))
     return (
         jnp.asarray(np.stack(right).astype(jnp.bfloat16)),
-        jnp.asarray(np.stack(left).astype(jnp.bfloat16)),
+        jnp.asarray(np.stack(left[1:]).astype(jnp.bfloat16)),
     )
 
 
@@ -42,9 +42,9 @@
 
 def tile_kernel(
     phase_count, cells, intersection, slot_count, bits,
-    coef_ref, flags_ref, frames_ref, mask_ref, right_ref, left_ref, otf_ref, apod_ref, label_ref,
+    phase_ref, tiles_ref, frames_ref, mask_ref, right_ref, left_ref, otf_ref, apod_ref,
     out_ref,
-    wide_ref, gain_ref, images_ref, waves_ref, spec_ref, mid_ref, tile_ref, twin_ref, cand_ref,
+    label_ref, flip_ref, left0_ref, wide_ref, gain_ref, images_ref, waves_ref, spec_ref, mid_ref, tile_ref, twin_ref, cand_ref,
     names_ref, keep_ref, pack_ref, land_ref, hand_ref, final_ref, full_ref, up_ref, from_down_ref,
     from_right_ref, from_corner_ref, name_sems, twin_sems, cand_sems, pack_sems, final_sems, fold_sems,
 ):
@@ -110,6 +110,9 @@
         for target in greeted:
             pl.semaphore_signal(barrier, inc=1, device_id=target, device_id_type=pl.DeviceIdType.MESH)
         pl.semaphore_wait(barrier, len(greeted))
+        label_ref[...] = jnp.full(label_ref.shape, -1, jnp.int32)
+        for slot in range(slot_count):
+            label_ref[slot:slot + 1, :] = jnp.full((1, length), tiles_ref[slot], jnp.int32)
         for place in range(len(name_masks)):
             name_copy(place).start()
 
@@ -126,10 +129,24 @@
         wide_ref[0, :length, length:] = -neg_s
         wide_ref[0, length:, :length] = neg_s
         wide_ref[0, length:, length:] = c
+        left0_ref[:, :length] = c
+        left0_ref[:, length:] = -neg_s
+
+        index_sum = lax.broadcasted_iota(jnp.int32, (length, length), 0) + lax.broadcasted_iota(jnp.int32, (length, length), 1)
+        swap = jnp.where((index_sum == 0) | (index_sum == length), 1.0, 0.0).astype(jnp.bfloat16)
+        for place, source in enumerate((otf_ref, apod_ref)):
+            value = source[...]
+            high = value.astype(jnp.bfloat16)
+            rest = (value - high.astype(jnp.float32)).astype(jnp.bfloat16)
+            turned = None
+            for piece in (high, rest):
+                term = dot(dot(swap, piece).astype(jnp.bfloat16), swap)
+                turned = term if turned is None else turned + term
+            flip_ref[place] = turned
 
         for side in range(2):
             def rolled(m):
-                value = otf_ref[side]
+                value = otf_ref[...] if side == 0 else flip_ref[0]
                 if m == 0:
                     return value
                 value = pltpu.roll(value, (-m * shift_rows) % length, 0)
@@ -145,7 +162,7 @@
                     spec_side = value
                     mid_slot = halfway + m
                     gain_ref[mid_slot] = spec_side
-            scale = apod_ref[side] / total
+            scale = (apod_ref[...] if side == 0 else flip_ref[1]) / total
             if side == 0:
                 for m in range(halfway + 1):
                     gain_ref[m] = gain_ref[m] * scale
@@ -154,9 +171,19 @@
                     gain_ref[m] = gain_ref[m] + gain_ref[halfway + m] * scale
 
     width = length // cells
+    spread = jnp.where(
+        lax.broadcasted_iota(jnp.int32, (cells, length), 1) // width
+        == lax.broadcasted_iota(jnp.int32, (cells, length), 0), 1.0, 0.0).astype(jnp.bfloat16)
+    mask_rows = dot(mask_ref[0, 0].astype(jnp.float32).astype(jnp.bfloat16), spread)
+    places = (lax.broadcasted_iota(jnp.int32, (8, 128), 0), lax.broadcasted_iota(jnp.int32, (8, 128), 1))
+    angles = places[0].astype(jnp.float32) * (
+        phase_ref[step] + places[1].astype(jnp.float32) * (2.0 * math.pi / phase_count))
+    coefs = (jnp.cos(angles) / phase_count, -jnp.sin(angles) / phase_count)
+    weights = [[[jnp.broadcast_to(coefs[side][m:m + 1, p:p + 1], (width, length)) for p in range(phase_count)]
+                for side in range(2)] for m in range(1, halfway + 1)]
     for cell in range(cells):
         rows = pl.ds(cell * width, width)
-        keep = mask_ref[0, cell:cell + 1, :].astype(jnp.float32)
+        keep = mask_rows[cell:cell + 1, :]
         planes = [frames_ref[0, 0, 0, p, rows, :].astype(jnp.float32) * keep for p in range(phase_count)]
         total = planes[0]
         for p in range(1, phase_count):
@@ -164,10 +191,10 @@
         images_ref[0, rows, :length] = (total * (1.0 / phase_count)).astype(jnp.bfloat16)
         for m in range(1, halfway + 1):
             for side in range(2):
-                base = ((step * (halfway + 1) + m) * 2 + side) * phase_count
-                total = planes[0] * coef_ref[base]
+                weight = weights[m - 1][side]
+                total = planes[0] * weight[0]
                 for p in range(1, phase_count):
-                    total = total + planes[p] * coef_ref[base + p]
+                    total = total + planes[p] * weight[p]
                 images_ref[m, rows, side * length:(side + 1) * length] = total.astype(jnp.bfloat16)
 
     @pl.when(step > 0)
@@ -191,7 +218,7 @@
         rows = pl.ds(third * chunk, chunk)
         total = None
         for m in range(halfway + 1):
-            band = dot(left_ref[m, rows, :], waves_ref[m])
+            band = dot(left_ref[m - 1, rows, :] if m else left0_ref[rows, :], waves_ref[m])
             gain = gain_ref[m, rows, :]
             term = jnp.concatenate([gain, gain], axis=1) * band
             total = term if total is None else total + term
@@ -203,9 +230,10 @@
         mid_ref[rows, :] = mid[:, :length]
         mid_ref[pl.ds(length + third * chunk, chunk), :] = mid[:, length:]
 
-    held = flags_ref[step * 3] > 0
-    row_last = flags_ref[step * 3 + 1] > 0
-    column_last = flags_ref[step * 3 + 2] > 0
+    tile = tiles_ref[step]
+    held = tile >= 0
+    row_last = tile >= (count - 1) * GROUP_COLS
+    column_last = lax.rem(jnp.maximum(tile, 0), GROUP_COLS) + GROUP_COLS * group == GROUP_COLS * groups - 1
 
     def ramp(places, is_last):
         places = places.astype(jnp.float32) + 0.5
@@ -368,31 +396,18 @@
         fold_up.wait_send()
 
 
-def reversed_map(value):
-    return jnp.roll(value[::-1, ::-1], (1, 1), (0, 1))
-
-
-def stitched_block(frames, masks, phases, own_tiles, otf, apod, row_last, column_last, intersection):
+def stitched_block(frames, masks, phases, own_tiles, otf, apod, intersection):
     slot_count, phase_count = (frames.shape[1], frames.shape[3])
     length = otf.shape[0]
     cells = masks.shape[-1]
     halfway = phase_count // 2
-    orders = jnp.arange(0, halfway + 1).astype(jnp.float32)
-    phase_steps = jnp.arange(phase_count).astype(jnp.float32) * (2.0 * math.pi / phase_count)
-    angles = orders[None, :, None] * (phases[0] + phase_steps[None, :])[:, None, :]
-    coef = jnp.stack([jnp.cos(angles), -jnp.sin(angles)], axis=2) / phase_count
-    flags = jnp.stack([own_tiles >= 0, row_last, column_last], axis=1).astype(jnp.int32)
-    mask_rows = jnp.repeat(masks[0].astype(jnp.bfloat16), length // cells, axis=2)
     right, left = tables(length, halfway)
-    otfs = jnp.stack([otf, reversed_map(otf)])
-    apods = jnp.stack([apod, reversed_map(apod)])
     bands = halfway + 1
     count = lax.axis_size("ty")
     bits = count.bit_length() - 1
     part = length // 4
     wide = STRIDE * GROUP_COLS
     slot_rows = -(-slot_count // 8) * 8
-    names = jnp.broadcast_to(jnp.pad(own_tiles, (0, slot_rows - slot_count), constant_values=-1)[:, None], (slot_rows, length))
     most = GROUP_COLS << (bits - 2)
     dma = pltpu.SemaphoreType.DMA
 
@@ -406,12 +421,15 @@
             pl.BlockSpec(memory_space=pltpu.SMEM),
             pl.BlockSpec(memory_space=pltpu.SMEM),
             pl.BlockSpec((1, 1) + frames.shape[2:], lambda s: (0, s, 0, 0, 0, 0)),
-            pl.BlockSpec((1, cells, length), lambda s: (s, 0, 0)),
-            whole(right), whole(left), whole(otfs), whole(apods), whole(names),
+            pl.BlockSpec((1, 1, cells, cells), lambda s: (0, s, 0, 0)),
+            whole(right), whole(left), whole(otf), whole(apod),
         ],
         out_specs=pl.BlockSpec((STRIDE, wide), lambda s: (0, 0)),
         out_shape=jax.ShapeDtypeStruct((STRIDE, wide), jnp.float32),
         scratch_shapes=[
+            pltpu.VMEM((slot_rows, length), jnp.int32),
+            pltpu.VMEM((2, length, length), jnp.float32),
+            pltpu.VMEM((length, 2 * length), jnp.bfloat16),
             pltpu.VMEM((bands, 2 * length, 2 * length), jnp.bfloat16),
             pltpu.VMEM((2 * halfway + 1, length, length), jnp.float32),
             pltpu.VMEM((bands, length, 2 * length), jnp.bfloat16),
@@ -442,23 +460,15 @@
         compiler_params=pltpu.CompilerParams(
             vmem_limit_bytes=60 * 1024 * 1024, collective_id=0, has_side_effects=True
         ),
-    )(coef.reshape(-1), flags.reshape(-1), frames, mask_rows, right, left, otfs, apods, names)
+    )(phases.reshape(-1), own_tiles, frames, masks, right, left, otf, apod)
 
 
 def shards(frames, masks, phases, slot_tile, otf, apod):
-    row_count = lax.axis_size("ty")
-    group_count = lax.axis_size("tx")
-    my_group = lax.axis_index("tx")
     length = otf.shape[0]
     intersection = length - STRIDE
     own_tiles = slot_tile[0]
 
-    tile_rows = own_tiles // GROUP_COLS
-    columns = GROUP_COLS * my_group + own_tiles % GROUP_COLS
-    return stitched_block(
-        frames, masks, phases, own_tiles, otf, apod,
-        tile_rows == row_count - 1, columns == GROUP_COLS * group_count - 1, intersection,
-    )
+    return stitched_block(frames, masks, phases, own_tiles, otf, apod, intersection)
 
 
 def solution(mesh):

time: 58.6 us -> 49 us (0.84)
  local copies, waits for them, and re-layouts: 9.97 us -> 3.42 us
  other arithmetic: 3.81 us -> 0 us
  Pallas kernels: 44.5 us -> 45.3 us
    slice x10 -> x0, local copies, waits for them, and re-layouts: 4.91 us -> none  [reversed_map(): return jnp.roll(value[::-1, ::-1], (1, 1), (0, 1))]
    another operation x3 -> x0, other arithmetic: 2.15 us -> none  [the longest x2 1.88 us: stitched_block(): otfs = jnp.stack([otf, reversed_map(otf)])]
    unnamed x10 -> x2, local copies, waits for them, and re-layouts: 2.12 us -> 3.42 us
    pallas_call x1, Pallas kernels: 44.5 us -> 45.3 us  [stitched_block(): pl.pallas_call(lambda *refs: tile_kernel(phase_count, cells, intersection...]
    broadcast_in_dim x2 -> x0, local copies, waits for them, and re-layouts: 0.81 us -> none  [the longest x1 0.67 us: stitched_block(): jnp.broadcast_to(jnp.pad(own_tiles, (0, slot_rows - slot_count), constant...]
    reshape x1 -> x0, local copies, waits for them, and re-layouts: 0.76 us -> none  [stitched_block(): jnp.repeat(masks[0].astype(jnp.bfloat16), length // cells, axis=2)]
    convert_element_type x2 -> x0, local copies, waits for them, and re-layouts: 0.74 us -> none  [stitched_block(): jnp.stack([own_tiles >= 0, row_last, column_last], axis=1).astype(jnp.int32)]
    add x1 -> x0, other arithmetic: 0.72 us -> none  [stitched_block(): phases[0] + phase_steps[None, :]]
where the time goes in v3:
time: 49 us; the launch traced here: 48.8 us
  Pallas kernels  45.3 us (92%)
  local copies, waits for them, and re-layouts  3.42 us (7%)
    pallas_call x1, Pallas kernels, stitched_block(): pl.pallas_call(lambda *refs: tile_kernel(phase_count, cells, intersection...  45.3 us
    unnamed x2, local copies, waits for them, and re-layouts  3.42 us

profile of v3, /device:TPU:0, one launch (start us, length us, event | category | flops | bytes accessed | tf_op | source)
XLA Modules:
  0.0 48.8 jit_solution(11559419816968972271)
XLA Ops:
  0.0 1.3 %copy.9.refs_3_ = s32[1,3,12,12]{3,2,1,0:T(8,128)} copy(s32[1,3,12,12]{3,0,2,1:T(1,128)} %param.9) | data formatting | bytes 3456 | tf_op args[1]
  1.3 45.3 %shard_map.82 = f32[320,640]{1,0:T(8,128)} custom-call(f32[3]{0:T(128)} %bitcast.2, s32[3]{0:T(128)} %bitcast.3, bf16[1,3,1,5,384,384]{5,4,3,2,1,0:T(8,128)(2,1)} %refs_2_.1, s32[1,3,12,12]{3,2,1,0:T(8,128)} %copy.9.refs_3_, bf16[3,384,768]{2,1,0:T(8,128)(2,1)} %constant.4.clone.refs_4_, bf16[2,384,768]{2,1,0:T(8,128)(2,1)} %constant.5.clone.refs_5_, ...), custom_call_target="tpu_custom_call" | custom-call | tf_op jit(solution)/shard_map/pallas_call | solution.py:417
  46.7 2.1 %copy.11 = f32[320,640]{1,0:T(8,128)} copy(f32[320,640]{1,0:T(8,128)} %shard_map.82) | data formatting | bytes 1638400

commit v4 on v3

--- a/solution.py
+++ b/solution.py
@@ -42,9 +42,9 @@
 
 def tile_kernel(
     phase_count, cells, intersection, slot_count, bits,
-    phase_ref, tiles_ref, frames_ref, mask_ref, right_ref, left_ref, otf_ref, apod_ref,
+    phase_ref, tiles_ref, frames_ref, mask_ref, right_hbm, left_hbm, otf_ref, apod_ref,
     out_ref,
-    label_ref, flip_ref, left0_ref, wide_ref, gain_ref, images_ref, waves_ref, spec_ref, mid_ref, tile_ref, twin_ref, cand_ref,
+    table_sems, right_ref, left_ref, label_ref, flip_ref, left0_ref, wide_ref, gain_ref, images_ref, waves_ref, spec_ref, mid_ref, tile_ref, twin_ref, cand_ref,
     names_ref, keep_ref, pack_ref, land_ref, hand_ref, final_ref, full_ref, up_ref, from_down_ref,
     from_right_ref, from_corner_ref, name_sems, twin_sems, cand_sems, pack_sems, final_sems, fold_sems,
 ):
@@ -109,29 +109,11 @@
         barrier = pltpu.get_barrier_semaphore()
         for target in greeted:
             pl.semaphore_signal(barrier, inc=1, device_id=target, device_id_type=pl.DeviceIdType.MESH)
-        pl.semaphore_wait(barrier, len(greeted))
-        label_ref[...] = jnp.full(label_ref.shape, -1, jnp.int32)
-        for slot in range(slot_count):
-            label_ref[slot:slot + 1, :] = jnp.full((1, length), tiles_ref[slot], jnp.int32)
-        for place in range(len(name_masks)):
-            name_copy(place).start()
+        pltpu.make_async_copy(right_hbm, right_ref, table_sems.at[0]).start()
+        pltpu.make_async_copy(left_hbm, left_ref, table_sems.at[1]).start()
 
     @pl.when(step == 0)
     def _():
-        for m in range(1, halfway + 1):
-            c, neg_s = (right_ref[m, :, :length], right_ref[m, :, length:])
-            wide_ref[m, :length, :length] = c
-            wide_ref[m, :length, length:] = neg_s
-            wide_ref[m, length:, :length] = -neg_s
-            wide_ref[m, length:, length:] = c
-        c, neg_s = (right_ref[0, :, :length], right_ref[0, :, length:])
-        wide_ref[0, :length, :length] = c
-        wide_ref[0, :length, length:] = -neg_s
-        wide_ref[0, length:, :length] = neg_s
-        wide_ref[0, length:, length:] = c
-        left0_ref[:, :length] = c
-        left0_ref[:, length:] = -neg_s
-
         index_sum = lax.broadcasted_iota(jnp.int32, (length, length), 0) + lax.broadcasted_iota(jnp.int32, (length, length), 1)
         swap = jnp.where((index_sum == 0) | (index_sum == length), 1.0, 0.0).astype(jnp.bfloat16)
         for place, source in enumerate((otf_ref, apod_ref)):
@@ -169,6 +151,28 @@
             else:
                 for m in range(1, halfway + 1):
                     gain_ref[m] = gain_ref[m] + gain_ref[halfway + m] * scale
+
+        pl.semaphore_wait(pltpu.get_barrier_semaphore(), len(greeted))
+        label_ref[...] = jnp.full(label_ref.shape, -1, jnp.int32)
+        for slot in range(slot_count):
+            label_ref[slot:slot + 1, :] = jnp.full((1, length), tiles_ref[slot], jnp.int32)
+        for place in range(len(name_masks)):
+            name_copy(place).start()
+        pltpu.make_async_copy(right_hbm, right_ref, table_sems.at[0]).wait()
+        pltpu.make_async_copy(left_hbm, left_ref, table_sems.at[1]).wait()
+        for m in range(1, halfway + 1):
+            c, neg_s = (right_ref[m, :, :length], right_ref[m, :, length:])
+            wide_ref[m, :length, :length] = c
+            wide_ref[m, :length, length:] = neg_s
+            wide_ref[m, length:, :length] = -neg_s
+            wide_ref[m, length:, length:] = c
+        c, neg_s = (right_ref[0, :, :length], right_ref[0, :, length:])
+        wide_ref[0, :length, :length] = c
+        wide_ref[0, :length, length:] = -neg_s
+        wide_ref[0, length:, :length] = neg_s
+        wide_ref[0, length:, length:] = c
+        left0_ref[:, :length] = c
+        left0_ref[:, length:] = -neg_s
 
     width = length // cells
     spread = jnp.where(
@@ -278,63 +282,84 @@
                 masks = masks + [mask | (1 << bit) for mask in masks]
             return masks
 
-        def packed(piece, mask, column):
+        def packed(piece, mask, column, sources):
             wanted = across(mask)[1] * GROUP_COLS + column
             total = None
-            for slot in range(slot_count):
-                for who in range(4):
-                    hit = jnp.where(labels(piece, who, slot) == wanted, 1.0, 0.0).astype(jnp.bfloat16)
-                    term = candidate(piece, who, slot) * hit
-                    total = term if total is None else total + term
+            for slot, who in sources:
+                hit = jnp.where(labels(piece, who, slot) == wanted, 1.0, 0.0).astype(jnp.bfloat16)
+                term = candidate(piece, who, slot) * hit
+                total = term if total is None else total + term
             return total
 
-        def pack_copy(piece, hop):
-            size = GROUP_COLS << (len(routes[piece]) - hop)
+        def pack_copy(piece, hop, low):
+            size = GROUP_COLS << (len(routes[piece]) - hop - 1)
+            there = pl.ds(low * size, size)
             return sent(
-                pack_ref.at[piece, hop - 1, pl.ds(0, size)], land_ref.at[piece, hop - 1, pl.ds(0, size)],
-                pack_sems, (piece, hop - 1), across(1 << routes[piece][hop]),
+                pack_ref.at[piece, hop - 1, there], land_ref.at[piece, hop - 1, there],
+                pack_sems, (piece, hop - 1, low), across(1 << routes[piece][hop]),
             )
 
-        for piece in range(2):
-            for slot in range(slot_count):
+        def final_copy(piece):
+            return sent(hand_ref.at[piece], final_ref.at[piece], final_sems, (piece,), across(1))
+
+        last = slot_count - 1
+        early = [(slot, who) for slot in range(last) for who in range(4)] + [(last, 0), (last, 1)]
+        late = [(last, 2), (last, 3)]
+        rests = [combos(route[2:] + (0,)) for route in routes]
+        for piece in range(2):
+            for slot in range(last):
                 for who in range(2):
                     first_copy(slot, piece, who).wait_recv()
-            route = routes[piece]
-            rest = combos((0,) + route[2:])
-            for place, mask in enumerate(rest):
+        for piece in range(2):
+            for place, mask in enumerate(rests[piece]):
                 for column in range(GROUP_COLS):
-                    pack_ref[piece, 0, place * GROUP_COLS + column] = packed(piece, mask | (1 << route[1]), column)
-            pack_copy(piece, 1).start()
-        for piece in range(2):
-            for place, mask in enumerate(combos((0,) + routes[piece][2:])):
-                for column in range(GROUP_COLS):
-                    keep_ref[piece, place * GROUP_COLS + column] = packed(piece, mask, column)
-        for hop in range(1, bits - 1):
+                    index = place * GROUP_COLS + column
+                    pack_ref[piece, 0, index] = packed(piece, mask | (1 << routes[piece][1]), column, early)
+        for piece in range(2):
+            for who in range(2):
+                first_copy(last, piece, who).wait_recv()
+        for low in (1, 0):
             for piece in range(2):
-                pack_copy(piece, hop).wait_recv()
-                size = GROUP_COLS << (bits - 1 - hop)
-                if hop < bits - 2:
-                    held_order = combos((0,) + routes[piece][hop + 1:])
-                    later = combos((0,) + routes[piece][hop + 2:])
-                    bit = 1 << routes[piece][hop + 1]
-                    for place, mask in enumerate(later):
-                        there = held_order.index(mask | bit)
-                        here = held_order.index(mask)
+                for place, mask in enumerate(rests[piece]):
+                    if mask & 1 == low:
                         for column in range(GROUP_COLS):
-                            i, j, k = (there * GROUP_COLS + column, here * GROUP_COLS + column, place * GROUP_COLS + column)
-                            pack_ref[piece, hop, k] = keep_ref[piece, i] + land_ref[piece, hop - 1, i]
-                            keep_ref[piece, k] = keep_ref[piece, j] + land_ref[piece, hop - 1, j]
-                    pack_copy(piece, hop + 1).start()
-                else:
+                            index = place * GROUP_COLS + column
+                            pack_ref[piece, 0, index] = pack_ref[piece, 0, index] + packed(
+                                piece, mask | (1 << routes[piece][1]), column, late)
+                pack_copy(piece, 1, low).start()
+        for low in (1, 0):
+            for piece in range(2):
+                for place, mask in enumerate(rests[piece]):
+                    if mask & 1 == low:
+                        for column in range(GROUP_COLS):
+                            keep_ref[piece, place * GROUP_COLS + column] = packed(piece, mask, column, early + late)
+        for hop in range(1, bits - 2):
+            for piece in range(2):
+                for low in (1, 0):
+                    pack_copy(piece, hop, low).wait_recv()
+                held_order = combos(routes[piece][hop + 1:] + (0,))
+                bit = 1 << routes[piece][hop + 1]
+                for place, mask in enumerate(combos(routes[piece][hop + 2:] + (0,))):
+                    there = held_order.index(mask | bit)
+                    here = held_order.index(mask)
                     for column in range(GROUP_COLS):
-                        hand_ref[piece, column] = keep_ref[piece, GROUP_COLS + column] + land_ref[piece, hop - 1, GROUP_COLS + column]
-                    sent(hand_ref.at[piece], final_ref.at[piece], final_sems, (piece,), across(1)).start()
-        for piece in range(2):
+                        i, j, k = (there * GROUP_COLS + column, here * GROUP_COLS + column, place * GROUP_COLS + column)
+                        pack_ref[piece, hop, k] = keep_ref[piece, i] + land_ref[piece, hop - 1, i]
+                        keep_ref[piece, k] = keep_ref[piece, j] + land_ref[piece, hop - 1, j]
+                for low in (1, 0):
+                    pack_copy(piece, hop + 1, low).start()
+        for piece in range(2):
+            pack_copy(piece, bits - 2, 1).wait_recv()
+            for column in range(GROUP_COLS):
+                hand_ref[piece, column] = keep_ref[piece, GROUP_COLS + column] + land_ref[piece, bits - 3, GROUP_COLS + column]
+            final_copy(piece).start()
+        for piece in range(2):
+            pack_copy(piece, bits - 2, 0).wait_recv()
             rows = pl.ds(pl.multiple_of(own_rows + piece * part, part), part)
             for column in range(GROUP_COLS):
                 full_ref[column, rows, :] = keep_ref[piece, column] + land_ref[piece, bits - 3, column]
         for piece in range(2):
-            sent(hand_ref.at[piece], final_ref.at[piece], final_sems, (piece,), across(1)).wait_recv()
+            final_copy(piece).wait_recv()
             rows = pl.ds(pl.multiple_of(twin_rows + piece * part, part), part)
             for column in range(GROUP_COLS):
                 full_ref[column, rows, :] = final_ref[piece, column]
@@ -389,8 +414,9 @@
                     first_copy(slot, piece, who).wait_send()
         for piece in range(2):
             for hop in range(1, bits - 1):
-                pack_copy(piece, hop).wait_send()
-            sent(hand_ref.at[piece], final_ref.at[piece], final_sems, (piece,), across(1)).wait_send()
+                for low in range(2):
+                    pack_copy(piece, hop, low).wait_send()
+            final_copy(piece).wait_send()
         fold_left.wait_send()
         fold_corner.wait_send()
         fold_up.wait_send()
@@ -422,11 +448,14 @@
             pl.BlockSpec(memory_space=pltpu.SMEM),
             pl.BlockSpec((1, 1) + frames.shape[2:], lambda s: (0, s, 0, 0, 0, 0)),
             pl.BlockSpec((1, 1, cells, cells), lambda s: (0, s, 0, 0)),
-            whole(right), whole(left), whole(otf), whole(apod),
+            pl.BlockSpec(memory_space=pl.ANY), pl.BlockSpec(memory_space=pl.ANY), whole(otf), whole(apod),
         ],
         out_specs=pl.BlockSpec((STRIDE, wide), lambda s: (0, 0)),
         out_shape=jax.ShapeDtypeStruct((STRIDE, wide), jnp.float32),
         scratch_shapes=[
+            dma((2,)),
+            pltpu.VMEM(right.shape, jnp.bfloat16),
+            pltpu.VMEM(left.shape, jnp.bfloat16),
             pltpu.VMEM((slot_rows, length), jnp.int32),
             pltpu.VMEM((2, length, length), jnp.float32),
             pltpu.VMEM((length, 2 * length), jnp.bfloat16),
@@ -453,7 +482,7 @@
             dma((2, 5)),
             dma((2, slot_count)),
             dma((2, 2, slot_count, 2)),
-            dma((2, 2, bits - 2)),
+            dma((2, 2, bits - 2, 2)),
             dma((2, 2)),
             dma((2, 3)),
         ],

time: 49 us -> 44.6 us (0.910)
  Pallas kernels: 45.3 us -> 40.8 us
    pallas_call x1, Pallas kernels: 45.3 us -> 40.8 us  [stitched_block(): pl.pallas_call(lambda *refs: tile_kernel(phase_count, cells, intersection...]
where the time goes in v4:
time: 44.6 us; the launch traced here: 44.2 us
  Pallas kernels  40.8 us (91%)
  local copies, waits for them, and re-layouts  3.42 us (8%)
    pallas_call x1, Pallas kernels, stitched_block(): pl.pallas_call(lambda *refs: tile_kernel(phase_count, cells, intersection...  40.8 us
    unnamed x2, local copies, waits for them, and re-layouts  3.42 us

profile of v4, /device:TPU:0, one launch (start us, length us, event | category | flops | bytes accessed | tf_op | source)
XLA Modules:
  0.0 44.2 jit_solution(10013556618929073298)
XLA Ops:
  0.0 1.3 %copy.9.refs_3_ = s32[1,3,12,12]{3,2,1,0:T(8,128)} copy(s32[1,3,12,12]{3,0,2,1:T(1,128)} %param.9) | data formatting | bytes 3456 | tf_op args[1]
  1.3 40.8 %shard_map.82 = f32[320,640]{1,0:T(8,128)} custom-call(f32[3]{0:T(128)} %bitcast.2, s32[3]{0:T(128)} %bitcast.3, bf16[1,3,1,5,384,384]{5,4,3,2,1,0:T(8,128)(2,1)} %refs_2_.1, s32[1,3,12,12]{3,2,1,0:T(8,128)} %copy.9.refs_3_, bf16[3,384,768]{2,1,0:T(8,128)(2,1)} %constant.4.clone.refs_4_, bf16[2,384,768]{2,1,0:T(8,128)(2,1)} %constant.5.clone.refs_5_, ...), custom_call_target="tpu_custom_call" | custom-call | tf_op jit(solution)/shard_map/pallas_call | solution.py:443
  42.1 2.1 %copy.11 = f32[320,640]{1,0:T(8,128)} copy(f32[320,640]{1,0:T(8,128)} %shard_map.82) | data formatting | bytes 1638400

commit v5 on v4

--- a/solution.py
+++ b/solution.py
@@ -178,14 +178,14 @@
     spread = jnp.where(
         lax.broadcasted_iota(jnp.int32, (cells, length), 1) // width
         == lax.broadcasted_iota(jnp.int32, (cells, length), 0), 1.0, 0.0).astype(jnp.bfloat16)
-    mask_rows = dot(mask_ref[0, 0].astype(jnp.float32).astype(jnp.bfloat16), spread)
+    mask_rows = dot(mask_ref[0, :, 0, :].astype(jnp.float32).astype(jnp.bfloat16), spread)
     places = (lax.broadcasted_iota(jnp.int32, (8, 128), 0), lax.broadcasted_iota(jnp.int32, (8, 128), 1))
     angles = places[0].astype(jnp.float32) * (
         phase_ref[step] + places[1].astype(jnp.float32) * (2.0 * math.pi / phase_count))
     coefs = (jnp.cos(angles) / phase_count, -jnp.sin(angles) / phase_count)
     weights = [[[jnp.broadcast_to(coefs[side][m:m + 1, p:p + 1], (width, length)) for p in range(phase_count)]
                 for side in range(2)] for m in range(1, halfway + 1)]
-    for cell in range(cells):
+    def mix(cell):
         rows = pl.ds(cell * width, width)
         keep = mask_rows[cell:cell + 1, :]
         planes = [frames_ref[0, 0, 0, p, rows, :].astype(jnp.float32) * keep for p in range(phase_count)]
@@ -201,14 +201,12 @@
                     total = total + planes[p] * weight[p]
                 images_ref[m, rows, side * length:(side + 1) * length] = total.astype(jnp.bfloat16)
 
-    @pl.when(step > 0)
-    def _():
-        relay(step - 1)
-
-    for m in range(halfway + 1):
-        for third in range(3):
-            rows = pl.ds(third * chunk, chunk)
-            lower = pl.ds(length + third * chunk, chunk)
+    for third in range(3):
+        rows = pl.ds(third * chunk, chunk)
+        lower = pl.ds(length + third * chunk, chunk)
+        for cell in range(third * cells // 3, (third + 1) * cells // 3):
+            mix(cell)
+        for m in range(halfway + 1):
             if m == 0:
                 wave = dot(images_ref[0, rows, :length], right_ref[0])
             else:
@@ -217,6 +215,10 @@
             waves_ref[m, rows, :] = wave
             waves_ref[m, lower, :length] = wave[:, length:]
             waves_ref[m, lower, length:] = -wave[:, :length]
+
+    @pl.when(step > 0)
+    def _():
+        relay(step - 1)
 
     for third in range(3):
         rows = pl.ds(third * chunk, chunk)
@@ -447,7 +449,7 @@
             pl.BlockSpec(memory_space=pltpu.SMEM),
             pl.BlockSpec(memory_space=pltpu.SMEM),
             pl.BlockSpec((1, 1) + frames.shape[2:], lambda s: (0, s, 0, 0, 0, 0)),
-            pl.BlockSpec((1, 1, cells, cells), lambda s: (0, s, 0, 0)),
+            pl.BlockSpec((1, cells, 1, cells), lambda s: (s, 0, 0, 0)),
             pl.BlockSpec(memory_space=pl.ANY), pl.BlockSpec(memory_space=pl.ANY), whole(otf), whole(apod),
         ],
         out_specs=pl.BlockSpec((STRIDE, wide), lambda s: (0, 0)),
@@ -489,7 +491,7 @@
         compiler_params=pltpu.CompilerParams(
             vmem_limit_bytes=60 * 1024 * 1024, collective_id=0, has_side_effects=True
         ),
-    )(phases.reshape(-1), own_tiles, frames, masks, right, left, otf, apod)
+    )(phases.reshape(-1), own_tiles, frames, masks[0][:, :, None, :], right, left, otf, apod)
 
 
 def shards(frames, masks, phases, slot_tile, otf, apod):

time: 44.6 us -> 41.6 us (0.933)
  Pallas kernels: 40.8 us -> 39.2 us
  local copies, waits for them, and re-layouts: 3.42 us -> 2.09 us
    pallas_call x1, Pallas kernels: 40.8 us -> 39.2 us  [stitched_block(): pl.pallas_call(lambda *refs: tile_kernel(phase_count, cells, intersection...]
    unnamed x2 -> x1, local copies, waits for them, and re-layouts: 3.42 us -> 2.09 us
where the time goes in v5:
time: 41.6 us; the launch traced here: 41.3 us
  Pallas kernels  39.2 us (94%)
  local copies, waits for them, and re-layouts  2.09 us (5%)
    pallas_call x1, Pallas kernels, stitched_block(): pl.pallas_call(lambda *refs: tile_kernel(phase_count, cells, intersection...  39.2 us
    unnamed x1, local copies, waits for them, and re-layouts  2.09 us

profile of v5, /device:TPU:0, one launch (start us, length us, event | category | flops | bytes accessed | tf_op | source)
XLA Modules:
  0.0 41.3 jit_solution(6312019991752969358)
XLA Ops:
  0.0 39.2 %shard_map.82 = f32[320,640]{1,0:T(8,128)} custom-call(f32[3]{0:T(128)} %bitcast.4, s32[3]{0:T(128)} %bitcast.5, bf16[1,3,1,5,384,384]{5,4,3,2,1,0:T(8,128)(2,1)} %refs_2_.1, s32[3,12,1,12]{3,2,1,0:T(1,128)} %bitcast.3, bf16[3,384,768]{2,1,0:T(8,128)(2,1)} %constant.4.clone.refs_4_, bf16[2,384,768]{2,1,0:T(8,128)(2,1)} %constant.5.clone.refs_5_, ...), custom_call_target="tpu_custom_call" | custom-call | tf_op jit(solution)/shard_map/pallas_call | solution.py:445
  39.2 2.1 %copy.10 = f32[320,640]{1,0:T(8,128)} copy(f32[320,640]{1,0:T(8,128)} %shard_map.82) | data formatting | bytes 1638400
